TPU v7x, 32 devices: a whole 2x2x4 slice. The times are simulated.
32 devices in a mesh: dp: 8 (over z, core), mp: 4 (over y, x).
Axes of the slice: x: 2, y: 2, z: 4, core: 2. Of those that a mesh axis runs over, the one named last changes fastest.
Arguments:
- stream: bfloat16 [1152, 2640], P('dp'), may hold values from -6 to 6
- embedding: bfloat16 [1152, 2640], P('dp'), may hold values from -6 to 6
- cotangent: bfloat16 [1152, 2640], P('dp'), may hold values from -6 to 6
- norm_gain: float32 [2640], replicated, may hold values from 0.1 to 1.9
- up_weight: bfloat16 [2640, 8960], P('dp', 'mp'), may hold values from -0.125 to 0.125
- down_weight: bfloat16 [8960, 2640], P('mp', 'dp'), may hold values from -0.0625 to 0.0625
- counts: int32 [384], P('dp'), may hold values from 0 to 2, as said below
- destination: int32 [384], P('dp'), may hold values from 0 to 383, as said below
Outputs:
- new_stream: bfloat16 [1152, 2640], P('dp')
- embed_grad: bfloat16 [1152, 2640], P('dp')
Inputs may be any that keep to these rules, and one draw needn't show every extreme that they name: `counts`: A quarter of the indices of dp hold only blocks with a positive count; every other index holds 16 such blocks. `destination`: A permutation of the 384 block positions. Every index of dp sends the same number of blocks to every index of dp (a position p belongs to index p // 48), and exactly 24 blocks with a positive count are sent to each index.
All inputs are finite; a program needn't handle non-finite values.
Results may differ from a plain program's by a relative error of at most 0.02.
Values may be sent and summed in bfloat16 or wider, within the bound.
A program may use at most 128 MiB of HBM per device.

v0:
```python
import jax
import jax.numpy as jnp
from jax import lax
from jax.sharding import PartitionSpec as P

EPSILON = 1e-05


def layer_input(current, embedding, norm_gain):
    values = current.astype(jnp.float32)
    square = jnp.mean(values * values, axis=-1, keepdims=True)
    mixed = values * lax.rsqrt(square + EPSILON) * norm_gain + embedding.astype(jnp.float32)
    return mixed.astype(jnp.bfloat16)


def run_forward(current, embedding, row_counts, norm_gain, up_full, down_full):
    pre_last = None
    for iteration in range(2):
        layer_in = layer_input(current, embedding, norm_gain)
        pre_act = jnp.dot(layer_in, up_full, preferred_element_type=jnp.float32)
        activation = jax.nn.silu(pre_act).astype(jnp.bfloat16)
        partial_value = jnp.dot(activation, down_full, preferred_element_type=jnp.float32)
        update = lax.psum(partial_value.astype(jnp.bfloat16), "mp").astype(jnp.float32)
        advanced = (current.astype(jnp.float32) + update).astype(jnp.bfloat16)
        current = jnp.where((row_counts > iteration)[:, None], advanced, current)
        pre_last = pre_act
    return (current, pre_last)


def embed_gradient(cot_rows, pre_last, row_counts, up_full, down_full):
    grad_act = lax.dot_general(
        cot_rows, down_full, (((1,), (1,)), ((), ())), preferred_element_type=jnp.float32
    )
    sigmoid_pre = jax.nn.sigmoid(pre_last)
    grad_pre = (grad_act * (sigmoid_pre * (1.0 + pre_last * (1.0 - sigmoid_pre)))).astype(
        jnp.bfloat16
    )
    partial_value = lax.dot_general(
        grad_pre, up_full, (((1,), (1,)), ((), ())), preferred_element_type=jnp.float32
    )
    summed = lax.psum(partial_value.astype(jnp.bfloat16), "mp").astype(jnp.float32)
    return jnp.where((row_counts > 1)[:, None], summed, 0.0).astype(jnp.bfloat16)


def take_blocks(selector, block_data):
    return jnp.dot(
        selector.astype(jnp.bfloat16), block_data, preferred_element_type=jnp.float32
    ).astype(jnp.bfloat16)


def take_numbers(selector, numbers):
    return jnp.sum(jnp.where(selector, numbers[None, :], 0), axis=1).astype(jnp.int32)


def shards(stream, embedding, cotangent, norm_gain, up_weight, down_weight, counts, destination):
    up_full, down_full = (
        lax.all_gather(up_weight, "dp", axis=0, tiled=True),
        lax.all_gather(down_weight, "dp", axis=1, tiled=True),
    )
    row_total, feature_count = stream.shape
    blocks = counts.shape[0]
    block_rows = row_total // blocks
    block_width = block_rows * feature_count
    peer_count = lax.axis_size("dp")
    per_peer = blocks // peer_count
    peer_width = per_peer * block_width
    numbered = jnp.arange(blocks, dtype=jnp.int32)
    target = destination // blocks
    dest_slot = destination % blocks
    same_target = target[:, None] == target[None, :]
    earlier = numbered[None, :] < numbered[:, None]
    peer_rank = jnp.sum(same_target & earlier, axis=1)
    position = target * per_peer + peer_rank
    send_pick = position[None, :] == numbered[:, None]
    sent_slot = take_numbers(send_pick, dest_slot)
    stream_blocks = stream.reshape(blocks, block_width)
    embed_blocks = embedding.reshape(blocks, block_width)
    cot_blocks = cotangent.reshape(blocks, block_width)
    sent_count = take_numbers(send_pick, counts)
    sent_stream = take_blocks(send_pick, stream_blocks).reshape(peer_count, peer_width)
    sent_embed = take_blocks(send_pick, embed_blocks).reshape(peer_count, peer_width)
    got_stream, got_embed, got_count, got_slot = (
        lax.all_to_all(sent_stream, "dp", split_axis=0, concat_axis=0, tiled=True),
        lax.all_to_all(sent_embed, "dp", split_axis=0, concat_axis=0, tiled=True),
        lax.all_to_all(
            sent_count.reshape(peer_count, per_peer), "dp", split_axis=0, concat_axis=0, tiled=True
        ),
        lax.all_to_all(
            sent_slot.reshape(peer_count, per_peer), "dp", split_axis=0, concat_axis=0, tiled=True
        ),
    )
    got_stream = got_stream.reshape(blocks, block_width)
    got_embed = got_embed.reshape(blocks, block_width)
    got_count = got_count.reshape(blocks)
    got_slot = got_slot.reshape(blocks)
    capacity = blocks // 2
    live_mask = got_count > 0
    live_rank = jnp.cumsum(live_mask.astype(jnp.int32)) - 1
    compact_pick = live_mask[None, :] & (
        live_rank[None, :] == jnp.arange(capacity, dtype=jnp.int32)[:, None]
    )
    comp_stream = take_blocks(compact_pick, got_stream)
    comp_embed = take_blocks(compact_pick, got_embed)
    comp_count = take_numbers(compact_pick, got_count)
    comp_slot = take_numbers(compact_pick, got_slot)
    slot_pick = comp_slot[:, None] == numbered[None, :]
    comp_cot = take_blocks(slot_pick, cot_blocks)
    compact_rows = capacity * block_rows
    row_counts = jnp.repeat(comp_count, block_rows)
    new_rows, pre_last = run_forward(
        comp_stream.reshape(compact_rows, feature_count),
        comp_embed.reshape(compact_rows, feature_count),
        row_counts,
        norm_gain,
        up_full,
        down_full,
    )
    comp_grad = embed_gradient(
        comp_cot.reshape(compact_rows, feature_count), pre_last, row_counts, up_full, down_full
    )
    spread_pick = slot_pick.T
    place_pick = got_slot[None, :] == numbered[:, None]
    base_stream = take_blocks(place_pick, got_stream)
    live_slot = jnp.any(spread_pick, axis=1)
    spread_stream = take_blocks(spread_pick, new_rows.reshape(capacity, block_width))
    final_stream = jnp.where(live_slot[:, None], spread_stream, base_stream)
    final_grad = take_blocks(spread_pick, comp_grad.reshape(capacity, block_width))
    return (
        final_stream.reshape(row_total, feature_count),
        final_grad.reshape(row_total, feature_count),
    )


def solution(mesh):
    return jax.shard_map(
        shards,
        mesh=mesh,
        in_specs=(
            P("dp", None),
            P("dp", None),
            P("dp", None),
            P(),
            P("dp", "mp"),
            P("mp", "dp"),
            P("dp"),
            P("dp"),
        ),
        out_specs=(P("dp", None), P("dp", None)),
        check_vma=False,
    )
```

profile of v0, /device:TPU:0, one launch (start us, length us, event | category | flops | bytes accessed | tf_op | source)
XLA Modules:
  0.0 442.7 jit_solution(5021520385684813520)
XLA Ops:
  11.0 6.4 %all-to-all-start = ((s32[8,1,6]{2,1,0:T(1,128)}), s32[8,1,6]{2,1,0:T(1,128)S(1)}, u32[]{:S(2)}, u32[]{:S(2)}) async-start(s32[8,1,6]{2,1,0:T(1,128)} %bitcast), calls=%async_computation | async-start | bytes 8192 | tf_op jit(solution)/shard_map/all_to_all | solution.py:85
  19.9 2.9 all-to-all-done
  22.8 3.3 all-to-all-start.1
  28.5 5.3 %reduce.18 = bf16[8,47520]{1,0:T(8,128)(2,1)S(1)} reduce(bf16[8,1,47520]{2,1,0:T(2,128)(2,1)S(1)} %all_to_all.32, bf16[]{:T(256)} %broadcast.114), dimensions={1}, to_apply=%all_to_all.32.reduce_sub_computation | reduce | bytes 1520642 | tf_op jit(solution)/shard_map/all_to_all | solution.py:83
  35.3 5.5 %all-to-all-start.2 = ((bf16[8,2,23760]{2,1,0:T(2,128)(2,1)}), bf16[8,2,23760]{2,1,0:T(2,128)(2,1)S(1)}, u32[]{:S(2)}, u32[]{:S(2)}) async-start(bf16[8,2,23760]{2,1,0:T(2,128)(2,1)} %reshape.194), calls=%async_computation.2 | async-start | bytes 1523712 | tf_op jit(solution)/shard_map/all_to_all | solution.py:83
  43.5 5.3 %reduce.19 = bf16[8,47520]{1,0:T(8,128)(2,1)S(1)} reduce(bf16[8,1,47520]{2,1,0:T(2,128)(2,1)S(1)} %all_to_all.33, bf16[]{:T(256)} %broadcast.114), dimensions={1}, to_apply=%all_to_all.33.reduce_sub_computation | reduce | bytes 1520642 | tf_op jit(solution)/shard_map/all_to_all | solution.py:84
  50.4 29.6 %all-to-all-done.2 = bf16[8,2,23760]{2,1,0:T(2,128)(2,1)S(1)} async-done(((bf16[8,2,23760]{2,1,0:T(2,128)(2,1)}), bf16[8,2,23760]{2,1,0:T(2,128)(2,1)S(1)}, u32[]{:S(2)}, u32[]{:S(2)}) %all-to-all-start.2) | async-done | bytes 760352 | tf_op jit(solution)/shard_map/all_to_all | solution.py:83
  80.0 4.2 all-to-all-start.3
  84.5 2.5 reshape.159
  91.4 4.6 %reduce.5 = bf16[8,47520]{1,0:T(8,128)(2,1)S(1)} reduce(bf16[8,1,47520]{2,1,0:T(2,128)(2,1)S(1)} %reshape.195, bf16[]{:T(256)} %constant.52), dimensions={1}, to_apply=%all_to_all.29.reduce_sub_computation | reduce | bytes 1520642 | tf_op jit(solution)/shard_map/all_to_all | solution.py:83
  97.8 27.5 %all-to-all-done.3 = bf16[8,2,23760]{2,1,0:T(2,128)(2,1)} async-done(((bf16[8,2,23760]{2,1,0:T(2,128)(2,1)}), bf16[8,2,23760]{2,1,0:T(2,128)(2,1)}, u32[]{:S(2)}, u32[]{:S(2)}) %all-to-all-start.3) | async-done | bytes 760352 | tf_op jit(solution)/shard_map/all_to_all | solution.py:84
  125.4 5.0 %reshape.197 = bf16[8,1,47520]{2,1,0:T(2,128)(2,1)S(1)} reshape(bf16[8,2,23760]{2,1,0:T(2,128)(2,1)} %all-to-all-done.3) | data formatting | bytes 1520640
  130.4 4.8 %reduce.6 = bf16[8,47520]{1,0:T(8,128)(2,1)S(1)} reduce(bf16[8,1,47520]{2,1,0:T(2,128)(2,1)S(1)} %reshape.197, bf16[]{:T(256)} %constant.52), dimensions={1}, to_apply=%all_to_all.31.reduce_sub_computation | reduce | bytes 1520642 | tf_op jit(solution)/shard_map/all_to_all | solution.py:84
  137.1 22.8 %all-gather.5.cloned.1.call-done = bf16[8,330,2240]{2,1,0:T(8,128)(2,1)} async-done(((bf16[1,330,2240]{2,1,0:T(8,128)(2,1)}), bf16[8,330,2240]{2,1,0:T(8,128)(2,1)}) %all-gather.5.cloned.1.call-update) | async-done | bytes 11827216 | tf_op jit(solution)/shard_map/all_gather | solution.py:57
  159.9 17.7 %reshape.166 = bf16[2640,2240]{1,0:T(8,128)(2,1)} reshape(bf16[8,330,2240]{2,1,0:T(8,128)(2,1)} %all-gather.5.cloned.1.call-done) | data formatting | bytes 23654400
  177.6 97.2 %all-gather.7.cloned.1.call-done = bf16[8,330,2240]{2,1,0:T(8,128)(2,1)} async-done(((bf16[1,330,2240]{2,1,0:T(8,128)(2,1)}), bf16[8,330,2240]{2,1,0:T(8,128)(2,1)}) %all-gather.7.cloned.1.call-update) | async-done | bytes 11827216 | tf_op jit(solution)/shard_map/all_gather | solution.py:58
  274.8 16.7 %reshape.168 = bf16[2640,2240]{1,0:T(8,128)(2,1)} reshape(bf16[8,330,2240]{2,1,0:T(8,128)(2,1)} %all-gather.7.cloned.1.call-done) | data formatting | bytes 23654400
  291.5 13.9 %convolution_convert_fusion.10 = bf16[72,2640]{1,0:T(8,128)(2,1)} fusion(bf16[2640,2240]{1,0:T(8,128)(2,1)} %reshape.168, bf16[2640,2240]{1,0:T(8,128)(2,1)} %reshape.166, f32[72,2640]{1,0:T(8,128)S(1)} %reshape.164, bf16[72,2640]{1,0:T(8,128)(2,1)S(1)} %reshape.154, f32[2640]{0:T(1024)S(1)} %copy-done.2, f32[72]{0:T(128)S(1)} %add_rsqrt_fusion.1), kind=kOutput, calls=%fused_computation.14 | convolution fusion | flops 1705063680 | bytes 25185888 | tf_op jit(solution)/shard_map/dot_general | solution.py:22
  306.8 41.1 %all-reduce.4.cloned.1.call-done = bf16[72,2640]{1,0:T(8,128)(2,1)} async-done(((bf16[72,2640]{1,0:T(8,128)(2,1)}), bf16[72,2640]{1,0:T(8,128)(2,1)}) %all-reduce.4.cloned.1.call-update) | async-done | bytes 380176 | tf_op jit(solution)/shard_map/psum | solution.py:23
  349.2 6.4 %fusion.15 = f32[72,2240]{1,0:T(8,128)S(1)} fusion(bf16[2640,2240]{1,0:T(8,128)(2,1)} %reshape.166, f32[72,2640]{1,0:T(8,128)S(1)} %reshape.164, bf16[72,2640]{1,0:T(8,128)(2,1)S(1)} %get-tuple-element.11, f32[72]{0:T(128)S(1)} %add_rsqrt_fusion, f32[2640]{0:T(1024)S(1)} %copy-done.2), kind=kOutput, calls=%fused_computation.37 | convolution fusion | flops 852508800 | bytes 13623648 | tf_op jit(solution)/shard_map/dot_general | solution.py:20
  355.6 8.9 %convolution_convert_fusion.9 = bf16[72,2640]{1,0:T(8,128)(2,1)} fusion(bf16[2640,2240]{1,0:T(8,128)(2,1)} %reshape.168, f32[72,2240]{1,0:T(8,128)S(1)} %fusion.15), kind=kOutput, calls=%fused_computation.13 | convolution fusion | flops 852554880 | bytes 12852480 | tf_op jit(solution)/shard_map/dot_general | solution.py:22
  364.5 14.3 %convolution_convert_fusion.8 = bf16[72,2640]{1,0:T(8,128)(2,1)} fusion(bf16[2640,2240]{1,0:T(8,128)(2,1)} %reshape.166, bf16[72,2640]{1,0:T(8,128)(2,1)S(1)} %reshape.160, bf16[2640,2240]{1,0:T(8,128)(2,1)} %reshape.168, f32[72,2240]{1,0:T(8,128)S(1)} %fusion.15), kind=kOutput, calls=%fused_computation.12 | convolution fusion | flops 1704758400 | bytes 25059840 | tf_op jit(solution)/shard_map/dot_general | solution.py:38
  379.1 48.5 %all-reduce.6.cloned.1.call-done = (bf16[72,2640]{1,0:T(8,128)(2,1)}, bf16[72,2640]{1,0:T(8,128)(2,1)}) async-done(((bf16[72,2640]{1,0:T(8,128)(2,1)}, bf16[72,2640]{1,0:T(8,128)(2,1)}), (bf16[72,2640]{1,0:T(8,128)(2,1)}, bf16[72,2640]{1,0:T(8,128)(2,1)})) %all-reduce.6.cloned.1.call-update) | async-done | bytes 760336 | tf_op jit(solution)/shard_map/psum | solution.py:23
  431.2 2.0 reshape.162
  (67 shorter events, 32.1 us)
Async XLA Ops:
  7.2 33.7 %copy-start.1 = (bf16[144,2640]{1,0:T(8,128)(2,1)S(1)}, bf16[144,2640]{1,0:T(8,128)(2,1)}, u32[]{:S(2)}) copy-start(bf16[144,2640]{1,0:T(8,128)(2,1)} %param.9) | copy-start | bytes 2280964
  7.2 152.7 %all-gather.5.cloned.1.call-start = ((), (), s32[]{:S(2)}) async-start(), calls=%async_computation.5 | async-start | bytes 13934592 | tf_op jit(solution)/shard_map/all_gather | solution.py:57
  7.9 266.9 %all-gather.7.cloned.1.call-start = ((), (), s32[]{:S(2)}) async-start(), calls=%async_computation.6 | async-start | bytes 13934592 | tf_op jit(solution)/shard_map/all_gather | solution.py:58
  11.0 11.9 %all-to-all-start = ((s32[8,1,6]{2,1,0:T(1,128)}), s32[8,1,6]{2,1,0:T(1,128)S(1)}, u32[]{:S(2)}, u32[]{:S(2)}) async-start(s32[8,1,6]{2,1,0:T(1,128)} %bitcast), calls=%async_computation | async-start | bytes 8192 | tf_op jit(solution)/shard_map/all_to_all | solution.py:85
  22.8 12.5 %all-to-all-start.1 = ((s32[8,1,6]{2,1,0:T(1,128)}), s32[8,1,6]{2,1,0:T(1,128)S(1)}, u32[]{:S(2)}, u32[]{:S(2)}) async-start(s32[8,1,6]{2,1,0:T(1,128)} %bitcast.1), calls=%async_computation.1 | async-start | bytes 8192 | tf_op jit(solution)/shard_map/all_to_all | solution.py:88
  35.3 44.7 %all-to-all-start.2 = ((bf16[8,2,23760]{2,1,0:T(2,128)(2,1)}), bf16[8,2,23760]{2,1,0:T(2,128)(2,1)S(1)}, u32[]{:S(2)}, u32[]{:S(2)}) async-start(bf16[8,2,23760]{2,1,0:T(2,128)(2,1)} %reshape.194), calls=%async_computation.2 | async-start | bytes 1523712 | tf_op jit(solution)/shard_map/all_to_all | solution.py:83
  80.0 45.3 %all-to-all-start.3 = ((bf16[8,2,23760]{2,1,0:T(2,128)(2,1)}), bf16[8,2,23760]{2,1,0:T(2,128)(2,1)}, u32[]{:S(2)}, u32[]{:S(2)}) async-start(bf16[8,2,23760]{2,1,0:T(2,128)(2,1)} %reshape.196), calls=%async_computation.3 | async-start | bytes 1523712 | tf_op jit(solution)/shard_map/all_to_all | solution.py:84
  84.3 263.6 %all-reduce.4.cloned.1.call-start = ((), (), s32[]{:S(2)}) async-start(), calls=%async_computation.4 | async-start | bytes 774144 | tf_op jit(solution)/shard_map/psum | solution.py:23
  177.6 113.9 %copy-start.2 = (f32[2640]{0:T(1024)S(1)}, f32[2640]{0:T(1024)}, u32[]{:S(2)}) copy-start(f32[2640]{0:T(1024)} %param.11) | copy-start | bytes 31684
  291.5 14.3 %copy-start = (bf16[48,7920]{1,0:T(8,128)(2,1)S(1)}, bf16[48,7920]{1,0:T(8,128)(2,1)}, u32[]{:S(2)}) copy-start(bf16[48,7920]{1,0:T(8,128)(2,1)} %reshape.159) | copy-start | bytes 2280964
  305.4 122.2 %all-reduce.6.cloned.1.call-start = ((), (), s32[]{:S(2)}) async-start(), calls=%async_computation.7 | async-start | bytes 1548288 | tf_op jit(solution)/shard_map/psum | solution.py:23
Sparse Core Ops, SparseCore 0:
  9.6 150.2 all-gather.4
  161.6 113.2 all-gather.6
  305.5 42.2 all-reduce.3
  379.0 48.5 all-reduce.5
where the time goes:
time: 450 us; the launch traced here: 443 us
  waiting for transfers between devices  271 us (60%)
  local copies, waits for them, and re-layouts  64 us (14%)
  matrix products  46.2 us (10%)
  other arithmetic  27.3 us (6%)
  starting transfers between devices  19.9 us (4%)
  between operations  14.2 us (3%)
    all_gather x1, waiting for transfers between devices, shards(): lax.all_gather(down_weight, 'dp', axis=1, tiled=True)  97.2 us
    psum x2, waiting for transfers between devices, run_forward(): lax.psum(partial_value.astype(jnp.bfloat16), 'mp').astype(jnp.float32)  89.6 us
    unnamed x12, local copies, waits for them, and re-layouts  44.4 us
    all_to_all x1, waiting for transfers between devices, shards(): lax.all_to_all(sent_stream, 'dp', split_axis=0, concat_axis=0, tiled=True)  29.6 us
    all_to_all x1, waiting for transfers between devices, shards(): lax.all_to_all(sent_embed, 'dp', split_axis=0, concat_axis=0, tiled=True)  27.5 us
    dot_general x2, matrix products, run_forward(): jnp.dot(activation, down_full, preferred_element_type=jnp.float32)  22.8 us
    all_gather x1, waiting for transfers between devices, shards(): lax.all_gather(up_weight, 'dp', axis=0, tiled=True)  22.8 us
    dot_general x1, matrix products, embed_gradient(): lax.dot_general(grad_pre, up_full, (((1,), (1,)), ((), ())), preferred_el...  14.3 us
  transfers between devices with their start and end apart: 8, of which 7 were waited for; matrix products, arithmetic and copies ran while one was open for 14% of the time, Pallas kernels for 0%

commit v1 on v0

--- a/solution.py
+++ b/solution.py
@@ -1,9 +1,107 @@
+import functools
+
 import jax
 import jax.numpy as jnp
 from jax import lax
+from jax.experimental import pallas as pl
+from jax.experimental.pallas import tpu as pltpu
 from jax.sharding import PartitionSpec as P
 
 EPSILON = 1e-05
+MESH = pl.DeviceIdType.MESH
+
+
+def sum_kernel(n, part_ref, out_ref, got, full, send_sem, recv_sem, share_sem, full_sem):
+    me = lax.axis_index("mp")
+    barrier = pltpu.get_barrier_semaphore()
+    for k in range(1, n):
+        peer = lax.rem(me + k, n)
+        pl.semaphore_signal(barrier, inc=1, device_id={"mp": peer}, device_id_type=MESH)
+    pl.semaphore_wait(barrier, n - 1)
+    scatter = []
+    for k in range(1, n):
+        peer = lax.rem(me + k, n)
+        scatter.append(
+            pltpu.make_async_remote_copy(
+                src_ref=part_ref.at[peer],
+                dst_ref=got.at[k],
+                send_sem=send_sem.at[k],
+                recv_sem=recv_sem.at[k],
+                device_id={"mp": peer},
+                device_id_type=MESH,
+            )
+        )
+        scatter[-1].start()
+    total = part_ref[me].astype(jnp.float32)
+    for k in range(1, n):
+        scatter[k - 1].wait_recv()
+        total = total + got[k].astype(jnp.float32)
+    full[0] = total.astype(full.dtype)
+    share = []
+    for k in range(1, n):
+        peer = lax.rem(me + k, n)
+        share.append(
+            pltpu.make_async_remote_copy(
+                src_ref=full.at[0],
+                dst_ref=full.at[k],
+                send_sem=share_sem.at[k],
+                recv_sem=full_sem.at[k],
+                device_id={"mp": peer},
+                device_id_type=MESH,
+            )
+        )
+        share[-1].start()
+    out_ref[me] = full[0]
+    for k in range(1, n):
+        share[k - 1].wait_recv()
+        out_ref[lax.rem(me + n - k, n)] = full[k]
+    for k in range(1, n):
+        scatter[k - 1].wait_send()
+        share[k - 1].wait_send()
+
+
+def sum_over_mp(value, collective_id):
+    n = lax.axis_size("mp")
+    rows, width = value.shape
+    if n == 1:
+        return value
+    each = -(-rows // n)
+    padded = jnp.pad(value, ((0, each * n - rows), (0, 0))) if each * n != rows else value
+    shape = (n, each, width)
+    vmem = pl.BlockSpec(memory_space=pltpu.VMEM)
+    out = pl.pallas_call(
+        functools.partial(sum_kernel, n),
+        out_shape=jax.ShapeDtypeStruct(shape, value.dtype),
+        in_specs=[vmem],
+        out_specs=vmem,
+        scratch_shapes=[pltpu.VMEM(shape, value.dtype)] * 2 + [pltpu.SemaphoreType.DMA((n,))] * 4,
+        compiler_params=pltpu.CompilerParams(collective_id=collective_id, has_side_effects=True),
+    )(padded.reshape(shape))
+    return out.reshape(each * n, width)[:rows]
+
+
+def chunked(value, parts):
+    return value.reshape(value.shape[0], parts, value.shape[1] // parts)
+
+
+def times_up(value, up_parts):
+    return jnp.einsum(
+        "rpk,pkf->rf", chunked(value, up_parts.shape[0]), up_parts,
+        preferred_element_type=jnp.float32,
+    )
+
+
+def times_up_transposed(value, up_parts):
+    out = jnp.einsum("rf,pkf->rpk", value, up_parts, preferred_element_type=jnp.float32)
+    return out.astype(jnp.bfloat16).reshape(value.shape[0], -1)
+
+
+def times_down(value, down_parts):
+    return times_up_transposed(value, down_parts)
+
+
+def times_down_transposed(value, down_parts):
+    return times_up(value, down_parts)
 
 
 def layer_input(current, embedding, norm_gain):
@@ -13,33 +111,30 @@
     return mixed.astype(jnp.bfloat16)
 
 
-def run_forward(current, embedding, row_counts, norm_gain, up_full, down_full):
-    pre_last = None
-    for iteration in range(2):
-        layer_in = layer_input(current, embedding, norm_gain)
-        pre_act = jnp.dot(layer_in, up_full, preferred_element_type=jnp.float32)
-        activation = jax.nn.silu(pre_act).astype(jnp.bfloat16)
-        partial_value = jnp.dot(activation, down_full, preferred_element_type=jnp.float32)
-        update = lax.psum(partial_value.astype(jnp.bfloat16), "mp").astype(jnp.float32)
-        advanced = (current.astype(jnp.float32) + update).astype(jnp.bfloat16)
-        current = jnp.where((row_counts > iteration)[:, None], advanced, current)
-        pre_last = pre_act
-    return (current, pre_last)
-
-
-def embed_gradient(cot_rows, pre_last, row_counts, up_full, down_full):
-    grad_act = lax.dot_general(
-        cot_rows, down_full, (((1,), (1,)), ((), ())), preferred_element_type=jnp.float32
-    )
+def run_core(current, embedding, cot_rows, row_counts, norm_gain, up_parts, down_parts):
+    grad_act = times_down_transposed(cot_rows, down_parts)
+    layer_in = layer_input(current, embedding, norm_gain)
+    activation = jax.nn.silu(times_up(layer_in, up_parts)).astype(jnp.bfloat16)
+    activation = lax.optimization_barrier(activation)
+    update = sum_over_mp(times_down(activation, down_parts), 0).astype(jnp.float32)
+    advanced = (current.astype(jnp.float32) + update).astype(jnp.bfloat16)
+    current = jnp.where((row_counts > 0)[:, None], advanced, current)
+    layer_in = layer_input(current, embedding, norm_gain)
+    pre_last = times_up(layer_in, up_parts)
+    activation = jax.nn.silu(pre_last).astype(jnp.bfloat16)
     sigmoid_pre = jax.nn.sigmoid(pre_last)
+    grad_act = lax.optimization_barrier(grad_act)
     grad_pre = (grad_act * (sigmoid_pre * (1.0 + pre_last * (1.0 - sigmoid_pre)))).astype(
         jnp.bfloat16
     )
-    partial_value = lax.dot_general(
-        grad_pre, up_full, (((1,), (1,)), ((), ())), preferred_element_type=jnp.float32
-    )
-    summed = lax.psum(partial_value.astype(jnp.bfloat16), "mp").astype(jnp.float32)
-    return jnp.where((row_counts > 1)[:, None], summed, 0.0).astype(jnp.bfloat16)
+    both = jnp.concatenate(
+        [times_down(activation, down_parts), times_up_transposed(grad_pre, up_parts)], axis=0
+    )
+    both = sum_over_mp(both, 1)
+    update, summed = both[: current.shape[0]], both[current.shape[0] :]
+    advanced = (current.astype(jnp.float32) + update.astype(jnp.float32)).astype(jnp.bfloat16)
+    last = (row_counts > 1)[:, None]
+    return jnp.where(last, advanced, current), jnp.where(last, summed, jnp.zeros_like(summed))
 
 
 def take_blocks(selector, block_data):
@@ -53,10 +148,8 @@
 
 
 def shards(stream, embedding, cotangent, norm_gain, up_weight, down_weight, counts, destination):
-    up_full, down_full = (
-        lax.all_gather(up_weight, "dp", axis=0, tiled=True),
-        lax.all_gather(down_weight, "dp", axis=1, tiled=True),
-    )
+    up_parts = lax.all_gather(up_weight, "dp", axis=0, tiled=False)
+    down_parts = lax.all_gather(down_weight.T, "dp", axis=0, tiled=False)
     row_total, feature_count = stream.shape
     blocks = counts.shape[0]
     block_rows = row_total // blocks
@@ -107,16 +200,14 @@
     comp_cot = take_blocks(slot_pick, cot_blocks)
     compact_rows = capacity * block_rows
     row_counts = jnp.repeat(comp_count, block_rows)
-    new_rows, pre_last = run_forward(
+    new_rows, comp_grad = run_core(
         comp_stream.reshape(compact_rows, feature_count),
         comp_embed.reshape(compact_rows, feature_count),
+        comp_cot.reshape(compact_rows, feature_count),
         row_counts,
         norm_gain,
-        up_full,
-        down_full,
-    )
-    comp_grad = embed_gradient(
-        comp_cot.reshape(compact_rows, feature_count), pre_last, row_counts, up_full, down_full
+        up_parts,
+        down_parts,
     )
     spread_pick = slot_pick.T
     place_pick = got_slot[None, :] == numbered[:, None]

time: 450 us -> 396 us (0.88)
  waiting for transfers between devices: 271 us -> 185 us
  Pallas kernels: 0 us -> 43.9 us
  local copies, waits for them, and re-layouts: 64 us -> 44.6 us
  matrix products: 46.2 us -> 51.5 us
    psum x2 -> x0, waiting for transfers between devices: 89.6 us -> none  [run_forward(): lax.psum(partial_value.astype(jnp.bfloat16), 'mp').astype(jnp.float32)]
    pallas_call x0 -> x2, Pallas kernels: none -> 43.9 us  [sum_over_mp(): pl.pallas_call(functools.partial(sum_kernel, n), out_shape=jax.ShapeDtype...]
    unnamed x12 -> x14, local copies, waits for them, and re-layouts: 44.4 us -> 10.6 us
    convert_element_type x0 -> x7, local copies, waits for them, and re-layouts: none -> 7.7 us  [the longest x3 7.25 us: run_core(): sum_over_mp(times_down(activation, down_parts), 0).astype(jnp.float32)]
    all_gather x2, waiting for transfers between devices: 120 us -> 126 us  [the longest x1 107 us: shards(): down_parts = lax.all_gather(down_weight.T, 'dp', axis=0, tiled=False)]
    dot_general x4 -> x6, matrix products: 43.5 us -> 46.6 us  [the longest x3 25.5 us: times_up_transposed(): jnp.einsum('rf,pkf->rpk', value, up_parts, preferred_element_type=jnp.flo...]
  transfers between devices with their start and end apart: 8 -> 6, of which waited for: 7 -> 5; matrix products, arithmetic and copies ran while one was open for 14% -> 15% of each run, Pallas kernels for 0% -> 0%
where the time goes in v1:
time: 396 us; the launch traced here: 389 us
  waiting for transfers between devices  185 us (47%)
  matrix products  51.5 us (13%)
  local copies, waits for them, and re-layouts  44.6 us (11%)
  Pallas kernels  43.9 us (11%)
  other arithmetic  30.1 us (8%)
  starting transfers between devices  19.7 us (5%)
  between operations  15 us (4%)
    all_gather x1, waiting for transfers between devices, shards(): down_parts = lax.all_gather(down_weight.T, 'dp', axis=0, tiled=False)  107 us
    pallas_call x2, Pallas kernels, sum_over_mp(): pl.pallas_call(functools.partial(sum_kernel, n), out_shape=jax.ShapeDtype...  43.9 us
    all_to_all x1, waiting for transfers between devices, shards(): lax.all_to_all(sent_stream, 'dp', split_axis=0, concat_axis=0, tiled=True)  27.7 us
    all_to_all x1, waiting for transfers between devices, shards(): lax.all_to_all(sent_embed, 'dp', split_axis=0, concat_axis=0, tiled=True)  26.8 us
    dot_general x3, matrix products, times_up_transposed(): jnp.einsum('rf,pkf->rpk', value, up_parts, preferred_element_type=jnp.flo...  25.5 us
    dot_general x3, matrix products, times_up(): jnp.einsum('rpk,pkf->rf', chunked(value, up_parts.shape[0]), up_parts, pr...  21 us
    all_gather x1, waiting for transfers between devices, shards(): up_parts = lax.all_gather(up_weight, 'dp', axis=0, tiled=False)  18.3 us
    all_to_all x2, other arithmetic, shards(): lax.all_to_all(sent_embed, 'dp', split_axis=0, concat_axis=0, tiled=True)  10.9 us
  transfers between devices with their start and end apart: 6, of which 5 were waited for; matrix products, arithmetic and copies ran while one was open for 15% of the time, Pallas kernels for 0%

profile of v1, /device:TPU:0, one launch (start us, length us, event | category | flops | bytes accessed | tf_op | source)
XLA Modules:
  0.0 389.4 jit_solution(5431894847810017931)
XLA Ops:
  11.0 6.4 %all-to-all-start = ((s32[8,1,6]{2,1,0:T(1,128)}), s32[8,1,6]{2,1,0:T(1,128)S(1)}, u32[]{:S(2)}, u32[]{:S(2)}) async-start(s32[8,1,6]{2,1,0:T(1,128)} %bitcast), calls=%async_computation | async-start | bytes 8192 | tf_op jit(solution)/shard_map/all_to_all | solution.py:178
  19.9 3.0 all-to-all-done
  22.8 3.3 all-to-all-start.1
  28.4 5.2 %reduce.19 = bf16[8,47520]{1,0:T(8,128)(2,1)S(1)} reduce(bf16[8,1,47520]{2,1,0:T(2,128)(2,1)S(1)} %all_to_all.32, bf16[]{:T(256)} %broadcast.133), dimensions={1}, to_apply=%all_to_all.32.reduce_sub_computation | reduce | bytes 1520642 | tf_op jit(solution)/shard_map/all_to_all | solution.py:176
  35.3 5.6 %all-to-all-start.2 = ((bf16[8,2,23760]{2,1,0:T(2,128)(2,1)}), bf16[8,2,23760]{2,1,0:T(2,128)(2,1)S(1)}, u32[]{:S(2)}, u32[]{:S(2)}) async-start(bf16[8,2,23760]{2,1,0:T(2,128)(2,1)} %reshape.267), calls=%async_computation.2 | async-start | bytes 1523712 | tf_op jit(solution)/shard_map/all_to_all | solution.py:176
  43.5 5.3 %reduce.18 = bf16[8,47520]{1,0:T(8,128)(2,1)S(1)} reduce(bf16[8,1,47520]{2,1,0:T(2,128)(2,1)S(1)} %all_to_all.33, bf16[]{:T(256)} %broadcast.133), dimensions={1}, to_apply=%all_to_all.33.reduce_sub_computation | reduce | bytes 1520642 | tf_op jit(solution)/shard_map/all_to_all | solution.py:177
  52.3 27.7 %all-to-all-done.2 = bf16[8,2,23760]{2,1,0:T(2,128)(2,1)S(1)} async-done(((bf16[8,2,23760]{2,1,0:T(2,128)(2,1)}), bf16[8,2,23760]{2,1,0:T(2,128)(2,1)S(1)}, u32[]{:S(2)}, u32[]{:S(2)}) %all-to-all-start.2) | async-done | bytes 760352 | tf_op jit(solution)/shard_map/all_to_all | solution.py:176
  80.0 4.4 %all-to-all-start.3 = ((bf16[8,2,23760]{2,1,0:T(2,128)(2,1)}), bf16[8,2,23760]{2,1,0:T(2,128)(2,1)}, u32[]{:S(2)}, u32[]{:S(2)}) async-start(bf16[8,2,23760]{2,1,0:T(2,128)(2,1)} %reshape.265), calls=%async_computation.3 | async-start | bytes 1523712 | tf_op jit(solution)/shard_map/all_to_all | solution.py:177
  91.7 4.6 %reduce.5 = bf16[8,47520]{1,0:T(8,128)(2,1)S(1)} reduce(bf16[8,1,47520]{2,1,0:T(2,128)(2,1)S(1)} %reshape.268, bf16[]{:T(256)} %constant.54), dimensions={1}, to_apply=%all_to_all.29.reduce_sub_computation | reduce | bytes 1520642 | tf_op jit(solution)/shard_map/all_to_all | solution.py:176
  98.8 26.8 %all-to-all-done.3 = bf16[8,2,23760]{2,1,0:T(2,128)(2,1)} async-done(((bf16[8,2,23760]{2,1,0:T(2,128)(2,1)}), bf16[8,2,23760]{2,1,0:T(2,128)(2,1)}, u32[]{:S(2)}, u32[]{:S(2)}) %all-to-all-start.3) | async-done | bytes 760352 | tf_op jit(solution)/shard_map/all_to_all | solution.py:177
  125.6 5.1 %reshape.266 = bf16[8,1,47520]{2,1,0:T(2,128)(2,1)S(1)} reshape(bf16[8,2,23760]{2,1,0:T(2,128)(2,1)} %all-to-all-done.3) | data formatting | bytes 1520640
  130.6 5.7 %reduce.6 = bf16[8,47520]{1,0:T(8,128)(2,1)} reduce(bf16[8,1,47520]{2,1,0:T(2,128)(2,1)S(1)} %reshape.266, bf16[]{:T(256)} %constant.54), dimensions={1}, to_apply=%all_to_all.31.reduce_sub_computation | reduce | bytes 1520642 | tf_op jit(solution)/shard_map/all_to_all | solution.py:177
  141.6 18.3 %all-gather.7.cloned.1.call-done = bf16[8,330,2240]{2,1,0:T(8,128)(2,1)} async-done(((bf16[1,330,2240]{2,1,0:T(8,128)(2,1)}), bf16[8,330,2240]{2,1,0:T(8,128)(2,1)}) %all-gather.7.cloned.1.call-update) | async-done | bytes 11827216 | tf_op jit(solution)/shard_map/all_gather | solution.py:151
  159.9 7.5 %multiply_convert_fusion.2 = bf16[72,2240]{1,0:T(8,128)(2,1)} fusion(bf16[8,330,2240]{2,1,0:T(8,128)(2,1)} %all-gather.7.cloned.1.call-done, bf16[72,8,330]{2,1,0:T(8,128)(2,1)S(1)} %fusion.4), kind=kOutput, calls=%fused_computation.35 | convolution fusion | flops 852364800 | bytes 12529920 | tf_op jit(solution)/shard_map/rpk,pkf->rf/dot_general | solution.py:88
  167.4 107.4 %all-gather.9.cloned.1.call-done = bf16[8,330,2240]{2,1,0:T(8,128)(2,1)} async-done(((bf16[1,330,2240]{2,1,0:T(8,128)(2,1)}), bf16[8,330,2240]{2,1,0:T(8,128)(2,1)}) %all-gather.9.cloned.1.call-update) | async-done | bytes 11827216 | tf_op jit(solution)/shard_map/all_gather | solution.py:152
  274.8 8.6 %convolution_convert_fusion.10 = bf16[72,8,330]{2,0,1:T(8,128)(2,1)S(1)} fusion(bf16[8,330,2240]{2,1,0:T(8,128)(2,1)} %all-gather.9.cloned.1.call-done, bf16[72,2240]{1,0:T(8,128)(2,1)} %multiply_convert_fusion.2), kind=kOutput, calls=%fused_computation.15 | convolution fusion | flops 851748480 | bytes 12529920 | tf_op jit(solution)/shard_map/rf,pkf->rpk/dot_general | solution.py:95
  284.9 19.3 %shard_map.95 = bf16[4,18,2640]{2,1,0:T(8,128)(2,1)} custom-call(bf16[4,18,2640]{2,1,0:T(8,128)(2,1)} %reshape_reshape.6.part_ref), custom_call_target="tpu_custom_call" | custom-call | tf_op jit(solution)/shard_map/pallas_call | solution.py:72
  306.3 2.9 reshape.223
  314.4 6.8 %convolution_bitcast_fusion.1 = f32[72,2240]{1,0:T(8,128)S(1)} fusion(bf16[8,330,2240]{2,1,0:T(8,128)(2,1)} %all-gather.7.cloned.1.call-done, bf16[72,8,330]{2,1,0:T(8,128)(2,1)S(1)} %add_convert_fusion), kind=kOutput, calls=%fused_computation.11 | convolution fusion | flops 851558400 | bytes 12852480 | tf_op jit(solution)/shard_map/rpk,pkf->rf/dot_general | solution.py:88
  321.2 8.4 %convolution_convert_fusion.9 = bf16[72,8,330]{2,0,1:T(8,128)(2,1)S(1)} fusion(bf16[8,330,2240]{2,1,0:T(8,128)(2,1)} %all-gather.9.cloned.1.call-done, f32[72,2240]{1,0:T(8,128)S(1)} %convolution_bitcast_fusion.1), kind=kOutput, calls=%fused_computation.14 | convolution fusion | flops 852554880 | bytes 12852480 | tf_op jit(solution)/shard_map/rf,pkf->rpk/dot_general | solution.py:95
  330.0 6.7 %convolution_bitcast_fusion = f32[72,2240]{1,0:T(8,128)S(1)} fusion(bf16[8,330,2240]{2,1,0:T(8,128)(2,1)} %all-gather.9.cloned.1.call-done, bf16[72,8,330]{2,1,0:T(8,128)(2,1)S(1)} %copy-done.1), kind=kOutput, calls=%fused_computation.10 | convolution fusion | flops 851558400 | bytes 12852480 | tf_op jit(solution)/shard_map/rpk,pkf->rf/dot_general | solution.py:88
  336.8 8.5 %convolution_convert_fusion.8 = bf16[72,8,330]{2,0,1:T(8,128)(2,1)S(1)} fusion(bf16[8,330,2240]{2,1,0:T(8,128)(2,1)} %all-gather.7.cloned.1.call-done, f32[72,2240]{1,0:T(8,128)S(1)} %convolution_bitcast_fusion, f32[72,2240]{1,0:T(8,128)S(1)} %convolution_bitcast_fusion.1), kind=kOutput, calls=%fused_computation.13 | convolution fusion | flops 853200000 | bytes 13497600 | tf_op jit(solution)/shard_map/rf,pkf->rpk/dot_general | solution.py:95
  346.9 24.6 %shard_map.96 = bf16[4,36,2640]{2,1,0:T(8,128)(2,1)} custom-call(bf16[4,36,2640]{2,1,0:T(8,128)(2,1)} %reshape.217.part_ref), custom_call_target="tpu_custom_call" | custom-call | tf_op jit(solution)/shard_map/pallas_call | solution.py:72
  375.9 2.3 reshape.218
  (79 shorter events, 50.0 us)
Async XLA Ops:
  7.2 33.7 %copy-start.2 = (bf16[144,2640]{1,0:T(8,128)(2,1)S(1)}, bf16[144,2640]{1,0:T(8,128)(2,1)}, u32[]{:S(2)}) copy-start(bf16[144,2640]{1,0:T(8,128)(2,1)} %param.9) | copy-start | bytes 2280964
  7.2 43.2 %copy-start.3 = (f32[2640]{0:T(1024)S(1)}, f32[2640]{0:T(1024)}, u32[]{:S(2)}) copy-start(f32[2640]{0:T(1024)} %param.11) | copy-start | bytes 31684
  7.2 152.8 %all-gather.7.cloned.1.call-start = ((), (), s32[]{:S(2)}) async-start(), calls=%async_computation.4 | async-start | bytes 13934592 | tf_op jit(solution)/shard_map/all_gather | solution.py:151
  7.9 266.9 %all-gather.9.cloned.1.call-start = ((), (), s32[]{:S(2)}) async-start(), calls=%async_computation.5 | async-start | bytes 13934592 | tf_op jit(solution)/shard_map/all_gather | solution.py:152
  11.0 11.9 %all-to-all-start = ((s32[8,1,6]{2,1,0:T(1,128)}), s32[8,1,6]{2,1,0:T(1,128)S(1)}, u32[]{:S(2)}, u32[]{:S(2)}) async-start(s32[8,1,6]{2,1,0:T(1,128)} %bitcast), calls=%async_computation | async-start | bytes 8192 | tf_op jit(solution)/shard_map/all_to_all | solution.py:178
  22.8 12.4 %all-to-all-start.1 = ((s32[8,1,6]{2,1,0:T(1,128)}), s32[8,1,6]{2,1,0:T(1,128)S(1)}, u32[]{:S(2)}, u32[]{:S(2)}) async-start(s32[8,1,6]{2,1,0:T(1,128)} %bitcast.1), calls=%async_computation.1 | async-start | bytes 8192 | tf_op jit(solution)/shard_map/all_to_all | solution.py:181
  35.3 44.8 %all-to-all-start.2 = ((bf16[8,2,23760]{2,1,0:T(2,128)(2,1)}), bf16[8,2,23760]{2,1,0:T(2,128)(2,1)S(1)}, u32[]{:S(2)}, u32[]{:S(2)}) async-start(bf16[8,2,23760]{2,1,0:T(2,128)(2,1)} %reshape.267), calls=%async_computation.2 | async-start | bytes 1523712 | tf_op jit(solution)/shard_map/all_to_all | solution.py:176
  80.0 45.5 %all-to-all-start.3 = ((bf16[8,2,23760]{2,1,0:T(2,128)(2,1)}), bf16[8,2,23760]{2,1,0:T(2,128)(2,1)}, u32[]{:S(2)}, u32[]{:S(2)}) async-start(bf16[8,2,23760]{2,1,0:T(2,128)(2,1)} %reshape.265), calls=%async_computation.3 | async-start | bytes 1523712 | tf_op jit(solution)/shard_map/all_to_all | solution.py:177
  86.9 0.5 copy-start.4
  314.4 15.7 %copy-start.1 = (bf16[72,8,330]{2,1,0:T(8,128)(2,1)S(1)}, bf16[72,8,330]{2,1,0:T(8,128)(2,1)}, u32[]{:S(2)}) copy-start(bf16[72,8,330]{2,1,0:T(8,128)(2,1)} %reshape_reshape.7) | copy-start | bytes 1140484
  336.8 37.0 %copy-start = (f32[24,7920]{1,0:T(8,128)S(1)}, f32[24,7920]{1,0:T(8,128)}, u32[]{:S(2)}) copy-start(f32[24,7920]{1,0:T(8,128)} %reshape.222) | copy-start | bytes 2280964
Sparse Core Ops, SparseCore 0:
  9.6 150.2 all-gather.6
  161.6 113.2 all-gather.8

commit v2 on v1

--- a/solution.py
+++ b/solution.py
@@ -58,6 +58,51 @@
     for k in range(1, n):
         scatter[k - 1].wait_send()
         share[k - 1].wait_send()
+
+
+def share_kernel(n, own_ref, out_ref, full, send_sem, recv_sem):
+    me = lax.axis_index("mp")
+    barrier = pltpu.get_barrier_semaphore()
+    for k in range(1, n):
+        peer = lax.rem(me + k, n)
+        pl.semaphore_signal(barrier, inc=1, device_id={"mp": peer}, device_id_type=MESH)
+    pl.semaphore_wait(barrier, n - 1)
+    share = []
+    for k in range(1, n):
+        peer = lax.rem(me + k, n)
+        share.append(
+            pltpu.make_async_remote_copy(
+                src_ref=own_ref,
+                dst_ref=full.at[k],
+                send_sem=send_sem.at[k],
+                recv_sem=recv_sem.at[k],
+                device_id={"mp": peer},
+                device_id_type=MESH,
+            )
+        )
+        share[-1].start()
+    out_ref[me] = own_ref[...]
+    for k in range(1, n):
+        share[k - 1].wait_recv()
+        out_ref[lax.rem(me + n - k, n)] = full[k]
+    for k in range(1, n):
+        share[k - 1].wait_send()
+
+
+def share_over_mp(value, collective_id):
+    n = lax.axis_size("mp")
+    if n == 1:
+        return value[None]
+    shape = (n,) + value.shape
+    vmem = pl.BlockSpec(memory_space=pltpu.VMEM)
+    return pl.pallas_call(
+        functools.partial(share_kernel, n),
+        out_shape=jax.ShapeDtypeStruct(shape, value.dtype),
+        in_specs=[vmem],
+        out_specs=vmem,
+        scratch_shapes=[pltpu.VMEM(shape, value.dtype)] + [pltpu.SemaphoreType.DMA((n,))] * 2,
+        compiler_params=pltpu.CompilerParams(collective_id=collective_id, has_side_effects=True),
+    )(value)
 
 
 def sum_over_mp(value, collective_id):
@@ -77,16 +122,19 @@
         scratch_shapes=[pltpu.VMEM(shape, value.dtype)] * 2 + [pltpu.SemaphoreType.DMA((n,))] * 4,
         compiler_params=pltpu.CompilerParams(collective_id=collective_id, has_side_effects=True),
     )(padded.reshape(shape))
-    return out.reshape(each * n, width)[:rows]
+    return lax.optimization_barrier(out.reshape(each * n, width)[:rows])
 
 
 def chunked(value, parts):
-    return value.reshape(value.shape[0], parts, value.shape[1] // parts)
+    value = lax.optimization_barrier(value)
+    return lax.optimization_barrier(value.reshape(value.shape[0], parts, value.shape[1] // parts))
 
 
 def times_up(value, up_parts):
     return jnp.einsum(
-        "rpk,pkf->rf", chunked(value, up_parts.shape[0]), up_parts,
+        "rpk,pkf->rf",
+        chunked(value, up_parts.shape[0]),
+        up_parts,
         preferred_element_type=jnp.float32,
     )
 
@@ -147,17 +195,23 @@
     return jnp.sum(jnp.where(selector, numbers[None, :], 0), axis=1).astype(jnp.int32)
 
 
+def rows_of(block_numbers, block_rows):
+    offsets = jnp.arange(block_rows, dtype=jnp.int32)
+    return (block_numbers[:, None] * block_rows + offsets[None, :]).reshape(-1)
+
+
 def shards(stream, embedding, cotangent, norm_gain, up_weight, down_weight, counts, destination):
     up_parts = lax.all_gather(up_weight, "dp", axis=0, tiled=False)
     down_parts = lax.all_gather(down_weight.T, "dp", axis=0, tiled=False)
     row_total, feature_count = stream.shape
     blocks = counts.shape[0]
     block_rows = row_total // blocks
-    block_width = block_rows * feature_count
     peer_count = lax.axis_size("dp")
     per_peer = blocks // peer_count
-    peer_width = per_peer * block_width
+    capacity = blocks // 2
     numbered = jnp.arange(blocks, dtype=jnp.int32)
+    row_numbered = jnp.arange(row_total, dtype=jnp.int32)
+    compact_numbered = jnp.arange(capacity * block_rows, dtype=jnp.int32)
     target = destination // blocks
     dest_slot = destination % blocks
     same_target = target[:, None] == target[None, :]
@@ -165,61 +219,58 @@
     peer_rank = jnp.sum(same_target & earlier, axis=1)
     position = target * per_peer + peer_rank
     send_pick = position[None, :] == numbered[:, None]
-    sent_slot = take_numbers(send_pick, dest_slot)
-    stream_blocks = stream.reshape(blocks, block_width)
-    embed_blocks = embedding.reshape(blocks, block_width)
-    cot_blocks = cotangent.reshape(blocks, block_width)
-    sent_count = take_numbers(send_pick, counts)
-    sent_stream = take_blocks(send_pick, stream_blocks).reshape(peer_count, peer_width)
-    sent_embed = take_blocks(send_pick, embed_blocks).reshape(peer_count, peer_width)
-    got_stream, got_embed, got_count, got_slot = (
-        lax.all_to_all(sent_stream, "dp", split_axis=0, concat_axis=0, tiled=True),
-        lax.all_to_all(sent_embed, "dp", split_axis=0, concat_axis=0, tiled=True),
-        lax.all_to_all(
-            sent_count.reshape(peer_count, per_peer), "dp", split_axis=0, concat_axis=0, tiled=True
-        ),
-        lax.all_to_all(
-            sent_slot.reshape(peer_count, per_peer), "dp", split_axis=0, concat_axis=0, tiled=True
-        ),
-    )
-    got_stream = got_stream.reshape(blocks, block_width)
-    got_embed = got_embed.reshape(blocks, block_width)
-    got_count = got_count.reshape(blocks)
-    got_slot = got_slot.reshape(blocks)
-    capacity = blocks // 2
+    sent_numbers = jnp.stack(
+        [
+            take_numbers(send_pick, counts).reshape(peer_count, per_peer),
+            take_numbers(send_pick, dest_slot).reshape(peer_count, per_peer),
+        ],
+        axis=1,
+    )
+    got_numbers = lax.all_to_all(sent_numbers, "dp", split_axis=0, concat_axis=0, tiled=True)
+    send_rows = rows_of(position, block_rows)[None, :] == row_numbered[:, None]
+    shares = lax.axis_size("mp")
+    share = feature_count // shares
+    start = lax.axis_index("mp") * share
+    own = jnp.concatenate(
+        [
+            lax.dynamic_slice_in_dim(stream, start, share, axis=1),
+            lax.dynamic_slice_in_dim(embedding, start, share, axis=1),
+        ],
+        axis=1,
+    )
+    sent = take_blocks(send_rows, own).reshape(peer_count, per_peer * block_rows, 2 * share)
+    got = lax.all_to_all(sent, "dp", split_axis=0, concat_axis=0, tiled=True)
+    got = share_over_mp(got.reshape(row_total, 2 * share), 2)
+    got_stream = jnp.concatenate([got[k, :, :share] for k in range(shares)], axis=1)
+    got_embed = jnp.concatenate([got[k, :, share:] for k in range(shares)], axis=1)
+    got_count = got_numbers[:, 0, :].reshape(blocks)
+    got_slot = got_numbers[:, 1, :].reshape(blocks)
     live_mask = got_count > 0
     live_rank = jnp.cumsum(live_mask.astype(jnp.int32)) - 1
     compact_pick = live_mask[None, :] & (
         live_rank[None, :] == jnp.arange(capacity, dtype=jnp.int32)[:, None]
     )
-    comp_stream = take_blocks(compact_pick, got_stream)
-    comp_embed = take_blocks(compact_pick, got_embed)
     comp_count = take_numbers(compact_pick, got_count)
     comp_slot = take_numbers(compact_pick, got_slot)
-    slot_pick = comp_slot[:, None] == numbered[None, :]
-    comp_cot = take_blocks(slot_pick, cot_blocks)
-    compact_rows = capacity * block_rows
-    row_counts = jnp.repeat(comp_count, block_rows)
+    compact_at = jnp.where(live_mask, live_rank, capacity)
+    compact_rows = rows_of(compact_at, block_rows)[None, :] == compact_numbered[:, None]
+    slot_rows = rows_of(comp_slot, block_rows)[:, None] == row_numbered[None, :]
+    place_rows = rows_of(got_slot, block_rows)[None, :] == row_numbered[:, None]
+    base_stream = lax.optimization_barrier(take_blocks(place_rows, got_stream))
     new_rows, comp_grad = run_core(
-        comp_stream.reshape(compact_rows, feature_count),
-        comp_embed.reshape(compact_rows, feature_count),
-        comp_cot.reshape(compact_rows, feature_count),
-        row_counts,
+        take_blocks(compact_rows, got_stream),
+        take_blocks(compact_rows, got_embed),
+        take_blocks(slot_rows, cotangent),
+        jnp.repeat(comp_count, block_rows),
         norm_gain,
         up_parts,
         down_parts,
     )
-    spread_pick = slot_pick.T
-    place_pick = got_slot[None, :] == numbered[:, None]
-    base_stream = take_blocks(place_pick, got_stream)
-    live_slot = jnp.any(spread_pick, axis=1)
-    spread_stream = take_blocks(spread_pick, new_rows.reshape(capacity, block_width))
-    final_stream = jnp.where(live_slot[:, None], spread_stream, base_stream)
-    final_grad = take_blocks(spread_pick, comp_grad.reshape(capacity, block_width))
-    return (
-        final_stream.reshape(row_total, feature_count),
-        final_grad.reshape(row_total, feature_count),
-    )
+    spread_rows = rows_of(comp_slot, block_rows)[None, :] == row_numbered[:, None]
+    live_rows = jnp.any(spread_rows, axis=1)
+    spread_stream = take_blocks(spread_rows, new_rows)
+    final_stream = jnp.where(live_rows[:, None], spread_stream, base_stream)
+    return final_stream, take_blocks(spread_rows, comp_grad)
 
 
 def solution(mesh):

time: 396 us -> 356 us (0.90); the launches traced: 389 us -> 355 us
  other arithmetic: 30.1 us -> 4.2 us
  local copies, waits for them, and re-layouts: 44.6 us -> 19.8 us
  Pallas kernels: 43.9 us -> 67 us
  starting transfers between devices: 19.7 us -> 9.97 us
    all_gather x1, waiting for transfers between devices: 18.3 us -> 49.1 us  [shards(): up_parts = lax.all_gather(up_weight, 'dp', axis=0, tiled=False)]
    all_to_all x4 -> x2, waiting for transfers between devices: 57.5 us -> 28.7 us  [the longest x1 25.9 us: shards(): got = lax.all_to_all(sent, 'dp', split_axis=0, concat_axis=0, tiled=True)]
    pallas_call x0 -> x1, Pallas kernels: none -> 23.1 us  [share_over_mp(): pl.pallas_call(functools.partial(share_kernel, n), out_shape=jax.ShapeDty...]
    all_to_all x6 -> x0, other arithmetic: 22.1 us -> none  [the longest x2 10.9 us: shards(): lax.all_to_all(sent_embed, 'dp', split_axis=0, concat_axis=0, tiled=True)]
    unnamed x14, local copies, waits for them, and re-layouts: 10.6 us -> 0.03 us
    all_to_all x4 -> x2, starting transfers between devices: 19.6 us -> 9.89 us  [the longest x1 6.35 us: shards(): lax.all_to_all(sent_numbers, 'dp', split_axis=0, concat_axis=0, tiled=True)]
    convert_element_type x5 -> x0, local copies, waits for them, and re-layouts: 9.18 us -> none  [the longest x3 7.25 us: run_core(): sum_over_mp(times_down(activation, down_parts), 0).astype(jnp.float32)]
    reshape x10 -> x7, local copies, waits for them, and re-layouts: 13.2 us -> 6.32 us  [the longest x2 2.71 us: sum_over_mp(): return lax.optimization_barrier(out.reshape(each * n, width)[:rows])]
  transfers between devices with their start and end apart: 6 -> 4, of which waited for: 5 -> 4; matrix products, arithmetic and copies ran while one was open for 15% -> 7% of each run, Pallas kernels for 0% -> 6%
where the time goes in v2:
time: 356 us; the launch traced here: 355 us
  waiting for transfers between devices  187 us (53%)
  Pallas kernels  67 us (19%)
  matrix products  52.7 us (15%)
  local copies, waits for them, and re-layouts  19.8 us (6%)
  between operations  14.4 us (4%)
  starting transfers between devices  9.97 us (3%)
  other arithmetic  4.2 us (1%)
    all_gather x1, waiting for transfers between devices, shards(): down_parts = lax.all_gather(down_weight.T, 'dp', axis=0, tiled=False)  108 us
    all_gather x1, waiting for transfers between devices, shards(): up_parts = lax.all_gather(up_weight, 'dp', axis=0, tiled=False)  49.1 us
    pallas_call x2, Pallas kernels, sum_over_mp(): pl.pallas_call(functools.partial(sum_kernel, n), out_shape=jax.ShapeDtype...  43.9 us
    all_to_all x1, waiting for transfers between devices, shards(): got = lax.all_to_all(sent, 'dp', split_axis=0, concat_axis=0, tiled=True)  25.9 us
    dot_general x3, matrix products, times_up_transposed(): jnp.einsum('rf,pkf->rpk', value, up_parts, preferred_element_type=jnp.flo...  25.5 us
    pallas_call x1, Pallas kernels, share_over_mp(): pl.pallas_call(functools.partial(share_kernel, n), out_shape=jax.ShapeDty...  23.1 us
    dot_general x3, matrix products, times_up(): jnp.einsum('rpk,pkf->rf', chunked(value, up_parts.shape[0]), up_parts, pr...  20.3 us
  transfers between devices with their start and end apart: 4, of which 4 were waited for; matrix products, arithmetic and copies ran while one was open for 7% of the time, Pallas kernels for 6%

profile of v2, /device:TPU:0, one launch (start us, length us, event | category | flops | bytes accessed | tf_op | source)
XLA Modules:
  0.0 355.4 jit_solution(2731571629219103371)
XLA Ops:
  11.1 6.4 %all-to-all-start = ((s32[8,2,6]{2,1,0:T(2,128)}), s32[8,2,6]{2,1,0:T(2,128)S(1)}, u32[]{:S(2)}, u32[]{:S(2)}) async-start(s32[8,2,6]{2,1,0:T(2,128)} %copy.28), calls=%async_computation | async-start | bytes 16384 | tf_op jit(solution)/shard_map/all_to_all | solution.py:229
  17.6 1.3 constant_dynamic-slice_fusion
  20.3 2.8 all-to-all-done
  23.1 3.5 all-to-all-start.1
  30.9 25.9 %all-to-all-done.1 = bf16[8,18,1320]{2,1,0:T(8,128)(2,1)S(1)} async-done(((bf16[8,18,1320]{2,1,0:T(8,128)(2,1)}), bf16[8,18,1320]{2,1,0:T(8,128)(2,1)S(1)}, u32[]{:S(2)}, u32[]{:S(2)}) %all-to-all-start.1) | async-done | bytes 380192 | tf_op jit(solution)/shard_map/all_to_all | solution.py:242
  57.8 23.1 %shard_map.95 = bf16[4,144,1320]{2,1,0:T(8,128)(2,1)} custom-call(bf16[144,1320]{1,0:T(8,128)(2,1)} %reshape.205.own_ref), custom_call_target="tpu_custom_call" | custom-call | tf_op jit(solution)/shard_map/pallas_call | solution.py:98
  80.8 2.8 slice_bitcast_fusion
  83.6 1.4 concatenate.13
  85.1 1.3 convolution_convert_fusion.1
  86.3 1.6 concatenate.14
  89.9 49.1 %all-gather.7.cloned.1.call-done = bf16[8,330,2240]{2,1,0:T(8,128)(2,1)} async-done(((bf16[1,330,2240]{2,1,0:T(8,128)(2,1)}), bf16[8,330,2240]{2,1,0:T(8,128)(2,1)}) %all-gather.7.cloned.1.call-update) | async-done | bytes 11827216 | tf_op jit(solution)/shard_map/all_gather | solution.py:204
  139.0 6.8 %multiply_convert_fusion.2 = bf16[72,2240]{1,0:T(8,128)(2,1)S(1)} fusion(bf16[8,330,2240]{2,1,0:T(8,128)(2,1)} %all-gather.7.cloned.1.call-done, bf16[72,8,330]{2,1,0:T(8,128)(2,1)S(1)} %reshape.206), kind=kOutput, calls=%fused_computation.35 | convolution fusion | flops 852364800 | bytes 12529920 | tf_op jit(solution)/shard_map/rpk,pkf->rf/dot_general | solution.py:134
  145.7 108.1 %all-gather.9.cloned.1.call-done = bf16[8,330,2240]{2,1,0:T(8,128)(2,1)} async-done(((bf16[1,330,2240]{2,1,0:T(8,128)(2,1)}), bf16[8,330,2240]{2,1,0:T(8,128)(2,1)}) %all-gather.9.cloned.1.call-update) | async-done | bytes 11827216 | tf_op jit(solution)/shard_map/all_gather | solution.py:205
  253.9 8.4 %convolution_convert_fusion.9 = bf16[72,8,330]{2,0,1:T(8,128)(2,1)S(1)} fusion(bf16[8,330,2240]{2,1,0:T(8,128)(2,1)} %all-gather.9.cloned.1.call-done, bf16[72,2240]{1,0:T(8,128)(2,1)S(1)} %multiply_convert_fusion.2), kind=kOutput, calls=%fused_computation.14 | convolution fusion | flops 851748480 | bytes 12529920 | tf_op jit(solution)/shard_map/rf,pkf->rpk/dot_general | solution.py:143
  262.4 1.4 reshape_reshape.3.part_ref
  263.8 19.3 %shard_map.96 = bf16[4,18,2640]{2,1,0:T(8,128)(2,1)} custom-call(bf16[4,18,2640]{2,1,0:T(8,128)(2,1)} %reshape_reshape.3.part_ref), custom_call_target="tpu_custom_call" | custom-call | tf_op jit(solution)/shard_map/pallas_call | solution.py:117
  284.3 6.7 %convolution_bitcast_fusion = f32[72,2240]{1,0:T(8,128)S(1)} fusion(bf16[8,330,2240]{2,1,0:T(8,128)(2,1)} %all-gather.9.cloned.1.call-done, bf16[72,8,330]{2,1,0:T(8,128)(2,1)S(1)} %reshape.210), kind=kOutput, calls=%fused_computation.4 | convolution fusion | flops 851558400 | bytes 12852480 | tf_op jit(solution)/shard_map/rpk,pkf->rf/dot_general | solution.py:134
  292.8 6.7 %convolution_bitcast_fusion.1 = f32[72,2240]{1,0:T(8,128)S(1)} fusion(bf16[8,330,2240]{2,1,0:T(8,128)(2,1)} %all-gather.7.cloned.1.call-done, bf16[72,8,330]{2,1,0:T(8,128)(2,1)S(1)} %reshape.208), kind=kOutput, calls=%fused_computation.5 | convolution fusion | flops 851558400 | bytes 12852480 | tf_op jit(solution)/shard_map/rpk,pkf->rf/dot_general | solution.py:134
  299.5 8.7 %convolution_convert_fusion.7 = bf16[72,8,330]{2,0,1:T(8,128)(2,1)S(1)} fusion(bf16[8,330,2240]{2,1,0:T(8,128)(2,1)} %all-gather.7.cloned.1.call-done, f32[72,2240]{1,0:T(8,128)S(1)} %convolution_bitcast_fusion, f32[72,2240]{1,0:T(8,128)S(1)} %convolution_bitcast_fusion.1), kind=kOutput, calls=%fused_computation.12 | convolution fusion | flops 853200000 | bytes 13497600 | tf_op jit(solution)/shard_map/rf,pkf->rpk/dot_general | solution.py:143
  308.6 8.4 %convolution_convert_fusion.8 = bf16[72,8,330]{2,0,1:T(8,128)(2,1)S(1)} fusion(bf16[8,330,2240]{2,1,0:T(8,128)(2,1)} %all-gather.9.cloned.1.call-done, f32[72,2240]{1,0:T(8,128)S(1)} %convolution_bitcast_fusion.1), kind=kOutput, calls=%fused_computation.13 | convolution fusion | flops 852554880 | bytes 12852480 | tf_op jit(solution)/shard_map/rf,pkf->rpk/dot_general | solution.py:143
  318.6 24.6 %shard_map.97 = bf16[4,36,2640]{2,1,0:T(8,128)(2,1)} custom-call(bf16[4,36,2640]{2,1,0:T(8,128)(2,1)} %reshape.212.part_ref), custom_call_target="tpu_custom_call" | custom-call | tf_op jit(solution)/shard_map/pallas_call | solution.py:117
  343.3 1.5 reshape.213
  344.8 1.3 convolution_convert_fusion
  346.1 2.5 fusion
  (72 shorter events, 17.3 us)
Async XLA Ops:
  7.2 21.4 %copy-start = (bf16[144,2640]{1,0:T(8,128)(2,1)S(1)}, bf16[144,2640]{1,0:T(8,128)(2,1)}, u32[]{:S(2)}) copy-start(bf16[144,2640]{1,0:T(8,128)(2,1)} %param.10) | copy-start | bytes 2280964
  7.2 81.2 %copy-start.1 = (f32[2640]{0:T(1024)S(1)}, f32[2640]{0:T(1024)}, u32[]{:S(2)}) copy-start(f32[2640]{0:T(1024)} %param.11) | copy-start | bytes 31684
  7.2 131.8 %all-gather.7.cloned.1.call-start = ((), (), s32[]{:S(2)}) async-start(), calls=%async_computation.2 | async-start | bytes 13934592 | tf_op jit(solution)/shard_map/all_gather | solution.py:204
  7.9 246.0 %all-gather.9.cloned.1.call-start = ((), (), s32[]{:S(2)}) async-start(), calls=%async_computation.3 | async-start | bytes 13934592 | tf_op jit(solution)/shard_map/all_gather | solution.py:205
  11.1 12.0 %all-to-all-start = ((s32[8,2,6]{2,1,0:T(2,128)}), s32[8,2,6]{2,1,0:T(2,128)S(1)}, u32[]{:S(2)}, u32[]{:S(2)}) async-start(s32[8,2,6]{2,1,0:T(2,128)} %copy.28), calls=%async_computation | async-start | bytes 16384 | tf_op jit(solution)/shard_map/all_to_all | solution.py:229
  23.1 33.8 %all-to-all-start.1 = ((bf16[8,18,1320]{2,1,0:T(8,128)(2,1)}), bf16[8,18,1320]{2,1,0:T(8,128)(2,1)S(1)}, u32[]{:S(2)}, u32[]{:S(2)}) async-start(bf16[8,18,1320]{2,1,0:T(8,128)(2,1)} %reshape.204), calls=%async_computation.1 | async-start | bytes 1081344 | tf_op jit(solution)/shard_map/all_to_all | solution.py:242
  27.7 60.7 %copy-start.3 = (s32[72]{0:T(128)}, s32[72]{0:T(128)S(1)}, u32[]{:S(2)}) copy-start(s32[72]{0:T(128)S(1)} %add.159) | copy-start | bytes 868
  27.8 60.5 %copy-start.2 = (s32[144]{0:T(256)}, s32[144]{0:T(256)S(1)}, u32[]{:S(2)}) copy-start(s32[144]{0:T(256)S(1)} %add.163) | copy-start | bytes 1732
  308.2 36.6 %copy-start.4 = (s32[72]{0:T(128)S(1)}, s32[72]{0:T(128)}, u32[]{:S(2)}) copy-start(s32[72]{0:T(128)} %copy-done.3) | copy-start | bytes 868
  308.2 36.6 %copy-start.5 = (pred[72]{0:T(512)(128)(4,1)S(1)}, pred[72]{0:T(512)(128)(4,1)}, u32[]{:S(2)}) copy-start(pred[72]{0:T(512)(128)(4,1)} %gt.53) | copy-start | bytes 220
  308.2 37.9 %copy-start.6 = (pred[144]{0:T(512)(128)(4,1)S(1)}, pred[144]{0:T(512)(128)(4,1)}, u32[]{:S(2)}) copy-start(pred[144]{0:T(512)(128)(4,1)} %fusion.30) | copy-start | bytes 436
Sparse Core Ops, SparseCore 0:
  9.6 129.2 all-gather.6
  140.6 113.2 all-gather.8

commit v3 on v2

--- a/solution.py
+++ b/solution.py
@@ -152,34 +152,53 @@
     return times_up(value, down_parts)
 
 
-def layer_input(current, embedding, norm_gain):
+def swap(value):
+    size = lax.axis_size("dp")
+    pairs = [(index, (index + size // 2) % size) for index in range(size)]
+    return lax.ppermute(value, "dp", pairs)
+
+
+def swap_sum(partial_value, own_rows):
+    other = swap(partial_value[own_rows:].astype(jnp.bfloat16))
+    return partial_value[:own_rows] + other.astype(jnp.float32)
+
+
+def both_rows(own):
+    return jnp.concatenate([own, swap(own)], axis=0)
+
+
+def layer_input(current, embedding, gain, own_rows, width):
     values = current.astype(jnp.float32)
-    square = jnp.mean(values * values, axis=-1, keepdims=True)
-    mixed = values * lax.rsqrt(square + EPSILON) * norm_gain + embedding.astype(jnp.float32)
+    square = jnp.sum(values * values, axis=-1)
+    other = swap(square)
+    square = square + jnp.concatenate([other[own_rows:], other[:own_rows]])
+    scale = lax.rsqrt(square / width + EPSILON)[:, None]
+    mixed = values * scale * gain + embedding.astype(jnp.float32)
     return mixed.astype(jnp.bfloat16)
 
 
-def run_core(current, embedding, cot_rows, row_counts, norm_gain, up_parts, down_parts):
-    grad_act = times_down_transposed(cot_rows, down_parts)
-    layer_in = layer_input(current, embedding, norm_gain)
-    activation = jax.nn.silu(times_up(layer_in, up_parts)).astype(jnp.bfloat16)
-    activation = lax.optimization_barrier(activation)
+def run_core(current, embedding, cot_rows, row_counts, gain, width, up_parts, down_parts):
+    own_rows = current.shape[0] // 2
+    layer_in = layer_input(current, embedding, gain, own_rows, width)
+    pre_act = swap_sum(times_up(layer_in, up_parts), own_rows)
+    activation = both_rows(jax.nn.silu(pre_act).astype(jnp.bfloat16))
+    grad_act = swap_sum(times_down_transposed(cot_rows, down_parts), own_rows)
     update = sum_over_mp(times_down(activation, down_parts), 0).astype(jnp.float32)
     advanced = (current.astype(jnp.float32) + update).astype(jnp.bfloat16)
     current = jnp.where((row_counts > 0)[:, None], advanced, current)
-    layer_in = layer_input(current, embedding, norm_gain)
-    pre_last = times_up(layer_in, up_parts)
-    activation = jax.nn.silu(pre_last).astype(jnp.bfloat16)
+    layer_in = layer_input(current, embedding, gain, own_rows, width)
+    pre_last = swap_sum(times_up(layer_in, up_parts), own_rows)
     sigmoid_pre = jax.nn.sigmoid(pre_last)
-    grad_act = lax.optimization_barrier(grad_act)
+    activation = both_rows((pre_last * sigmoid_pre).astype(jnp.bfloat16))
     grad_pre = (grad_act * (sigmoid_pre * (1.0 + pre_last * (1.0 - sigmoid_pre)))).astype(
         jnp.bfloat16
     )
+    grad_pre = both_rows(grad_pre)
     both = jnp.concatenate(
         [times_down(activation, down_parts), times_up_transposed(grad_pre, up_parts)], axis=0
     )
     both = sum_over_mp(both, 1)
-    update, summed = both[: current.shape[0]], both[current.shape[0] :]
+    update, summed = both[: 2 * own_rows], both[2 * own_rows :]
     advanced = (current.astype(jnp.float32) + update.astype(jnp.float32)).astype(jnp.bfloat16)
     last = (row_counts > 1)[:, None]
     return jnp.where(last, advanced, current), jnp.where(last, summed, jnp.zeros_like(summed))
@@ -200,13 +219,29 @@
     return (block_numbers[:, None] * block_rows + offsets[None, :]).reshape(-1)
 
 
+def for_pairs(value, halves=None):
+    half_size = value.shape[0] // 2
+    sides = value.reshape((2, half_size) + value.shape[1:])
+    picked = []
+    for side in range(2):
+        own, other = sides[side], sides[1 - side]
+        if halves is not None:
+            own, other = own[:, :, side], other[:, :, side]
+        picked.append(jnp.stack([own, other], axis=1))
+    return jnp.concatenate(picked, axis=0)
+
+
 def shards(stream, embedding, cotangent, norm_gain, up_weight, down_weight, counts, destination):
-    up_parts = lax.all_gather(up_weight, "dp", axis=0, tiled=False)
-    down_parts = lax.all_gather(down_weight.T, "dp", axis=0, tiled=False)
+    peer_count = lax.axis_size("dp")
+    half_peers = peer_count // 2
+    groups = [list(range(half_peers)), list(range(half_peers, peer_count))]
+    up_parts = lax.all_gather(up_weight, "dp", axis=0, tiled=False, axis_index_groups=groups)
+    down_parts = lax.all_gather(down_weight.T, "dp", axis=0, tiled=False, axis_index_groups=groups)
+    first = lax.axis_index("dp") < half_peers
     row_total, feature_count = stream.shape
+    half = feature_count // 2
     blocks = counts.shape[0]
     block_rows = row_total // blocks
-    peer_count = lax.axis_size("dp")
     per_peer = blocks // peer_count
     capacity = blocks // 2
     numbered = jnp.arange(blocks, dtype=jnp.int32)
@@ -226,46 +261,76 @@
         ],
         axis=1,
     )
-    got_numbers = lax.all_to_all(sent_numbers, "dp", split_axis=0, concat_axis=0, tiled=True)
+    got_numbers = lax.all_to_all(
+        for_pairs(sent_numbers), "dp", split_axis=0, concat_axis=0, tiled=True
+    )
     send_rows = rows_of(position, block_rows)[None, :] == row_numbered[:, None]
     shares = lax.axis_size("mp")
-    share = feature_count // shares
+    share = -(-half // shares)
     start = lax.axis_index("mp") * share
-    own = jnp.concatenate(
-        [
-            lax.dynamic_slice_in_dim(stream, start, share, axis=1),
-            lax.dynamic_slice_in_dim(embedding, start, share, axis=1),
-        ],
-        axis=1,
-    )
-    sent = take_blocks(send_rows, own).reshape(peer_count, per_peer * block_rows, 2 * share)
-    got = lax.all_to_all(sent, "dp", split_axis=0, concat_axis=0, tiled=True)
-    got = share_over_mp(got.reshape(row_total, 2 * share), 2)
-    got_stream = jnp.concatenate([got[k, :, :share] for k in range(shares)], axis=1)
-    got_embed = jnp.concatenate([got[k, :, share:] for k in range(shares)], axis=1)
-    got_count = got_numbers[:, 0, :].reshape(blocks)
-    got_slot = got_numbers[:, 1, :].reshape(blocks)
-    live_mask = got_count > 0
-    live_rank = jnp.cumsum(live_mask.astype(jnp.int32)) - 1
-    compact_pick = live_mask[None, :] & (
-        live_rank[None, :] == jnp.arange(capacity, dtype=jnp.int32)[:, None]
-    )
-    comp_count = take_numbers(compact_pick, got_count)
-    comp_slot = take_numbers(compact_pick, got_slot)
-    compact_at = jnp.where(live_mask, live_rank, capacity)
-    compact_rows = rows_of(compact_at, block_rows)[None, :] == compact_numbered[:, None]
+
+    def own_share(value):
+        sides = [value[:, :half], value[:, half:]]
+        sides = [jnp.pad(side, ((0, 0), (0, share * shares - half))) for side in sides]
+        return [lax.dynamic_slice_in_dim(side, start, share, axis=1) for side in sides]
+
+    own_stream, own_embed = own_share(stream), own_share(embedding)
+    own = jnp.concatenate([own_stream[0], own_embed[0], own_stream[1], own_embed[1]], axis=1)
+    peer_rows = per_peer * block_rows
+    sent = take_blocks(send_rows, own).reshape(peer_count, peer_rows, 2, 2 * share)
+    got = lax.all_to_all(
+        for_pairs(sent, 2), "dp", split_axis=0, concat_axis=0, tiled=True
+    )
+    got = got.transpose(1, 0, 2, 3).reshape(2 * row_total, 2 * share)
+    got = share_over_mp(got, 2)
+    got_stream = jnp.concatenate([got[k, :, :share] for k in range(shares)], axis=1)[:, :half]
+    got_embed = jnp.concatenate([got[k, :, share:] for k in range(shares)], axis=1)[:, :half]
+
+    def full_width(own_half, other_half):
+        left = jnp.where(first, own_half, other_half)
+        right = jnp.where(first, other_half, own_half)
+        return jnp.concatenate([left, right], axis=1)
+
+    streams, embeds, row_counts, slots = [], [], [], []
+    for side in range(2):
+        got_count = got_numbers[:, side, 0, :].reshape(blocks)
+        got_slot = got_numbers[:, side, 1, :].reshape(blocks)
+        live_mask = got_count > 0
+        live_rank = jnp.cumsum(live_mask.astype(jnp.int32)) - 1
+        compact_pick = live_mask[None, :] & (
+            live_rank[None, :] == jnp.arange(capacity, dtype=jnp.int32)[:, None]
+        )
+        compact_at = jnp.where(live_mask, live_rank, capacity)
+        compact_rows = rows_of(compact_at, block_rows)[None, :] == compact_numbered[:, None]
+        side_rows = slice(side * row_total, (side + 1) * row_total)
+        streams.append(take_blocks(compact_rows, got_stream[side_rows]))
+        embeds.append(take_blocks(compact_rows, got_embed[side_rows]))
+        row_counts.append(jnp.repeat(take_numbers(compact_pick, got_count), block_rows))
+        slots.append((take_numbers(compact_pick, got_slot), got_slot))
+    comp_slot, got_slot = slots[0]
     slot_rows = rows_of(comp_slot, block_rows)[:, None] == row_numbered[None, :]
     place_rows = rows_of(got_slot, block_rows)[None, :] == row_numbered[:, None]
-    base_stream = lax.optimization_barrier(take_blocks(place_rows, got_stream))
+    comp_cot = take_blocks(slot_rows, cotangent)
+    left_cot, right_cot = comp_cot[:, :half], comp_cot[:, half:]
+    own_cot = jnp.where(first, left_cot, right_cot)
+    other_cot = swap(jnp.where(first, right_cot, left_cot))
+    arrived = full_width(got_stream[:row_total], swap(got_stream[row_total:]))
+    base_stream = lax.optimization_barrier(take_blocks(place_rows, arrived))
+    gain = jnp.where(first, norm_gain[:half], norm_gain[half:])
     new_rows, comp_grad = run_core(
-        take_blocks(compact_rows, got_stream),
-        take_blocks(compact_rows, got_embed),
-        take_blocks(slot_rows, cotangent),
-        jnp.repeat(comp_count, block_rows),
-        norm_gain,
+        jnp.concatenate(streams, axis=0),
+        jnp.concatenate(embeds, axis=0),
+        jnp.concatenate([own_cot, other_cot], axis=0),
+        jnp.concatenate(row_counts, axis=0),
+        gain,
+        feature_count,
         up_parts,
         down_parts,
     )
+    own_rows = capacity * block_rows
+    other = swap(jnp.concatenate([new_rows[own_rows:], comp_grad[own_rows:]], axis=0))
+    new_rows = full_width(new_rows[:own_rows], other[:own_rows])
+    comp_grad = full_width(comp_grad[:own_rows], other[own_rows:])
     spread_rows = rows_of(comp_slot, block_rows)[None, :] == row_numbered[:, None]
     live_rows = jnp.any(spread_rows, axis=1)
     spread_stream = take_blocks(spread_rows, new_rows)

time: 356 us -> 334 us (0.938)
  waiting for transfers between devices: 187 us -> 165 us
  matrix products: 52.7 us -> 32.4 us
  starting transfers between devices: 9.97 us -> 23.5 us
  other arithmetic: 4.2 us -> 9.89 us
    all_gather x2, waiting for transfers between devices: 157 us -> 48.4 us  [the longest x1 47 us: shards(): lax.all_gather(down_weight.T, 'dp', axis=0, tiled=False, axis_index_group...]
    ppermute x0 -> x11, waiting for transfers between devices: none -> 101 us  [swap(): return lax.ppermute(value, 'dp', pairs)]
    all_to_all x2, waiting for transfers between devices: 28.7 us -> 14.3 us  [the longest x1 13.7 us: shards(): lax.all_to_all(for_pairs(sent, 2), 'dp', split_axis=0, concat_axis=0, til...]
    ppermute x0 -> x11, starting transfers between devices: none -> 12.5 us  [swap(): return lax.ppermute(value, 'dp', pairs)]
    dot_general x3, matrix products: 25.5 us -> 15.1 us  [times_up_transposed(): jnp.einsum('rf,pkf->rpk', value, up_parts, preferred_element_type=jnp.flo...]
    dot_general x3, matrix products: 20.3 us -> 12.3 us  [times_up(): jnp.einsum('rpk,pkf->rf', chunked(value, up_parts.shape[0]), up_parts, pr...]
  transfers between devices with their start and end apart: 4 -> 15, of which waited for: 4 -> 11; matrix products, arithmetic and copies ran while one was open for 7% -> 15% of each run, Pallas kernels for 6% -> 15%
where the time goes in v3:
time: 334 us
  waiting for transfers between devices  165 us (49%)
  Pallas kernels  66.8 us (20%)
  matrix products  32.4 us (10%)
  starting transfers between devices  23.5 us (7%)
  local copies, waits for them, and re-layouts  20.9 us (6%)
  between operations  14.7 us (4%)
  other arithmetic  9.89 us (3%)
    ppermute x11, waiting for transfers between devices, swap(): return lax.ppermute(value, 'dp', pairs)  101 us
    all_gather x1, waiting for transfers between devices, shards(): lax.all_gather(down_weight.T, 'dp', axis=0, tiled=False, axis_index_group...  47 us
    pallas_call x2, Pallas kernels, sum_over_mp(): pl.pallas_call(functools.partial(sum_kernel, n), out_shape=jax.ShapeDtype...  43 us
    pallas_call x1, Pallas kernels, share_over_mp(): pl.pallas_call(functools.partial(share_kernel, n), out_shape=jax.ShapeDty...  23.8 us
    dot_general x3, matrix products, times_up_transposed(): jnp.einsum('rf,pkf->rpk', value, up_parts, preferred_element_type=jnp.flo...  15.1 us
    all_to_all x1, waiting for transfers between devices, shards(): lax.all_to_all(for_pairs(sent, 2), 'dp', split_axis=0, concat_axis=0, til...  13.7 us
    ppermute x11, starting transfers between devices, swap(): return lax.ppermute(value, 'dp', pairs)  12.5 us
    dot_general x3, matrix products, times_up(): jnp.einsum('rpk,pkf->rf', chunked(value, up_parts.shape[0]), up_parts, pr...  12.3 us
  transfers between devices with their start and end apart: 15, of which 11 were waited for; matrix products, arithmetic and copies ran while one was open for 15% of the time, Pallas kernels for 15%

profile of v3, /device:TPU:0, one launch (start us, length us, event | category | flops | bytes accessed | tf_op | source)
XLA Modules:
  0.0 333.5 jit_solution(4180981777708385391)
XLA Ops:
  9.1 6.4 %all-to-all-start = ((s32[8,2,2,6]{3,2,1,0:T(2,128)}), s32[8,2,2,6]{3,2,1,0:T(2,128)S(1)}, u32[]{:S(2)}, u32[]{:S(2)}) async-start(s32[8,2,2,6]{3,2,1,0:T(2,128)} %copy.71), calls=%async_computation | async-start | bytes 32768 | tf_op jit(solution)/shard_map/all_to_all | solution.py:264
  21.1 4.6 %all-to-all-start.1 = ((bf16[8,2,18,660]{3,1,2,0:T(2,128)(2,1)}), bf16[8,2,18,660]{3,1,2,0:T(2,128)(2,1)S(1)}, u32[]{:S(2)}, u32[]{:S(2)}) async-start(bf16[8,2,18,660]{3,1,2,0:T(2,128)(2,1)} %copy.78), calls=%async_computation.1 | async-start | bytes 884736 | tf_op jit(solution)/shard_map/all_to_all | solution.py:281
  28.8 13.7 %all-to-all-done.1 = bf16[8,2,18,660]{3,1,2,0:T(2,128)(2,1)S(1)} async-done(((bf16[8,2,18,660]{3,1,2,0:T(2,128)(2,1)}), bf16[8,2,18,660]{3,1,2,0:T(2,128)(2,1)S(1)}, u32[]{:S(2)}, u32[]{:S(2)}) %all-to-all-start.1) | async-done | bytes 380192 | tf_op jit(solution)/shard_map/all_to_all | solution.py:281
  43.5 23.8 %shard_map.95 = bf16[4,288,660]{2,1,0:T(8,128)(2,1)} custom-call(bf16[288,660]{1,0:T(8,128)(2,1)} %reshape.318.own_ref), custom_call_target="tpu_custom_call" | custom-call | tf_op jit(solution)/shard_map/pallas_call | solution.py:98
  67.4 2.7 slice_bitcast_fusion
  71.3 3.3 collective-permute-start
  79.0 4.0 %convolution_bitcast_fusion.2 = f32[144,2240]{1,0:T(8,128)S(1)} fusion(bf16[4,330,2240]{2,1,0:T(8,128)(2,1)} %all-gather.7.cloned.1.call-done, bf16[144,4,330]{2,1,0:T(4,128)(2,1)S(1)} %reshape.319), kind=kOutput, calls=%fused_computation.2 | convolution fusion | flops 851558400 | bytes 7584000 | tf_op jit(solution)/shard_map/rpk,pkf->rf/dot_general | solution.py:134
  86.3 19.7 %collective-permute-done.1 = bf16[72,2240]{1,0:T(8,128)(2,1)S(1)} collective-permute-done((bf16[72,2240]{1,0:T(8,128)(2,1)S(1)}, bf16[72,2240]{1,0:T(8,128)(2,1)S(1)}, u32[]{:S(2)}, u32[]{:S(2)}) %collective-permute-start.1) | collective-permute-done | bytes 322592 | tf_op jit(solution)/shard_map/ppermute | solution.py:158
  106.3 4.9 %collective-permute-done.6 = bf16[72,1320]{1,0:T(8,128)(2,1)S(1)} collective-permute-done((bf16[72,1320]{1,0:T(8,128)(2,1)S(1)}, bf16[72,1320]{1,0:T(8,128)(2,1)S(1)}, u32[]{:S(2)}, u32[]{:S(2)}) %collective-permute-start.6) | collective-permute-done | bytes 190112 | tf_op jit(solution)/shard_map/ppermute | solution.py:158
  112.5 47.0 %all-gather.9.cloned.1.call-done = bf16[4,330,2240]{2,1,0:T(8,128)(2,1)} async-done(((bf16[1,330,2240]{2,1,0:T(8,128)(2,1)}), bf16[4,330,2240]{2,1,0:T(8,128)(2,1)}) %all-gather.9.cloned.1.call-update) | async-done | bytes 5913616 | tf_op jit(solution)/shard_map/all_gather | solution.py:239
  159.5 5.0 %convolution_convert_fusion.11 = bf16[144,4,330]{2,0,1:T(8,128)(2,1)S(1)} fusion(bf16[4,330,2240]{2,1,0:T(8,128)(2,1)} %all-gather.9.cloned.1.call-done, bf16[72,2240]{1,0:T(8,128)(2,1)} %collective-permute-done.2, bf16[72,2240]{1,0:T(8,128)(2,1)S(1)} %multiply_convert_fusion.1), kind=kOutput, calls=%fused_computation.15 | convolution fusion | flops 853038720 | bytes 6938880 | tf_op jit(solution)/shard_map/rf,pkf->rpk/dot_general | solution.py:143
  165.8 18.3 %shard_map.96 = bf16[4,36,1320]{2,1,0:T(8,128)(2,1)} custom-call(bf16[4,36,1320]{2,1,0:T(8,128)(2,1)} %reshape_reshape.4.part_ref), custom_call_target="tpu_custom_call" | custom-call | tf_op jit(solution)/shard_map/pallas_call | solution.py:117
  185.7 4.2 %convolution_bitcast_fusion = f32[144,2240]{1,0:T(8,128)S(1)} fusion(bf16[4,330,2240]{2,1,0:T(8,128)(2,1)} %all-gather.9.cloned.1.call-done, bf16[144,4,330]{2,1,0:T(4,128)(2,1)} %reshape.323), kind=kOutput, calls=%fused_computation | convolution fusion | flops 851558400 | bytes 7584000 | tf_op jit(solution)/shard_map/rpk,pkf->rf/dot_general | solution.py:134
  190.7 2.9 collective-permute-start.7
  196.9 4.1 %convolution_bitcast_fusion.1 = f32[144,2240]{1,0:T(8,128)S(1)} fusion(bf16[4,330,2240]{2,1,0:T(8,128)(2,1)} %all-gather.7.cloned.1.call-done, bf16[144,4,330]{2,1,0:T(4,128)(2,1)} %reshape.321), kind=kOutput, calls=%fused_computation.1 | convolution fusion | flops 851558400 | bytes 7584000 | tf_op jit(solution)/shard_map/rpk,pkf->rf/dot_general | solution.py:134
  201.3 15.6 %collective-permute-done.7 = bf16[72,2240]{1,0:T(8,128)(2,1)} collective-permute-done((bf16[72,2240]{1,0:T(8,128)(2,1)}, bf16[72,2240]{1,0:T(8,128)(2,1)}, u32[]{:S(2)}, u32[]{:S(2)}) %collective-permute-start.7) | collective-permute-done | bytes 322592 | tf_op jit(solution)/shard_map/ppermute | solution.py:158
  216.8 5.6 %collective-permute-done.4 = bf16[72,2240]{1,0:T(8,128)(2,1)S(1)} collective-permute-done((bf16[72,2240]{1,0:T(8,128)(2,1)S(1)}, bf16[72,2240]{1,0:T(8,128)(2,1)S(1)}, u32[]{:S(2)}, u32[]{:S(2)}) %collective-permute-start.4) | collective-permute-done | bytes 322592 | tf_op jit(solution)/shard_map/ppermute | solution.py:158
  225.7 2.9 collective-permute-start.10
  228.6 28.3 %collective-permute-done.8 = bf16[72,2240]{1,0:T(8,128)(2,1)S(1)} collective-permute-done((bf16[72,2240]{1,0:T(8,128)(2,1)}, bf16[72,2240]{1,0:T(8,128)(2,1)S(1)}, u32[]{:S(2)}, u32[]{:S(2)}) %collective-permute-start.8) | collective-permute-done | bytes 322592 | tf_op jit(solution)/shard_map/ppermute | solution.py:158
  257.0 5.0 %convolution_convert_fusion.9 = bf16[144,4,330]{2,0,1:T(8,128)(2,1)S(1)} fusion(bf16[4,330,2240]{2,1,0:T(8,128)(2,1)} %all-gather.7.cloned.1.call-done, bf16[72,2240]{1,0:T(8,128)(2,1)S(1)} %collective-permute-done.8, bf16[72,2240]{1,0:T(8,128)(2,1)} %get-tuple-element.24), kind=kOutput, calls=%fused_computation.13 | convolution fusion | flops 853038720 | bytes 6938880 | tf_op jit(solution)/shard_map/rf,pkf->rpk/dot_general | solution.py:143
  262.5 10.3 %collective-permute-done.5 = bf16[72,2240]{1,0:T(8,128)(2,1)} collective-permute-done((bf16[72,2240]{1,0:T(8,128)(2,1)}, bf16[72,2240]{1,0:T(8,128)(2,1)}, u32[]{:S(2)}, u32[]{:S(2)}) %collective-permute-start.5) | collective-permute-done | bytes 322592 | tf_op jit(solution)/shard_map/ppermute | solution.py:158
  272.8 5.2 %convolution_convert_fusion.10 = bf16[144,4,330]{2,0,1:T(8,128)(2,1)S(1)} fusion(bf16[4,330,2240]{2,1,0:T(8,128)(2,1)} %all-gather.9.cloned.1.call-done, bf16[72,2240]{1,0:T(8,128)(2,1)} %collective-permute-done.5, bf16[72,2240]{1,0:T(8,128)(2,1)S(1)} %copy-done.6), kind=kOutput, calls=%fused_computation.14 | convolution fusion | flops 853038720 | bytes 6938880 | tf_op jit(solution)/shard_map/rf,pkf->rpk/dot_general | solution.py:143
  279.5 24.6 %shard_map.97 = bf16[4,72,1320]{2,1,0:T(8,128)(2,1)} custom-call(bf16[4,72,1320]{2,1,0:T(8,128)(2,1)} %bitcast.65), custom_call_target="tpu_custom_call" | custom-call | tf_op jit(solution)/shard_map/pallas_call | solution.py:117
  307.2 16.9 %collective-permute-done.9 = bf16[144,1320]{1,0:T(8,128)(2,1)S(1)} collective-permute-done((bf16[144,1320]{1,0:T(8,128)(2,1)S(1)}, bf16[144,1320]{1,0:T(8,128)(2,1)S(1)}, u32[]{:S(2)}, u32[]{:S(2)}) %collective-permute-start.9) | collective-permute-done | bytes 380192 | tf_op jit(solution)/shard_map/ppermute | solution.py:158
  (146 shorter events, 39.8 us)
Async XLA Ops:
  7.2 20.5 %copy-start = (bf16[144,2640]{1,0:T(8,128)(2,1)S(1)}, bf16[144,2640]{1,0:T(8,128)(2,1)}, u32[]{:S(2)}) copy-start(bf16[144,2640]{1,0:T(8,128)(2,1)} %param.10) | copy-start | bytes 2280964
  7.2 1.0 copy-start.8
  7.2 71.8 %all-gather.7.cloned.1.call-start = ((), (), s32[]{:S(2)}) async-start(), calls=%async_computation.2 | async-start | bytes 7741440 | tf_op jit(solution)/shard_map/all_gather | solution.py:238
  7.2 9.2 %copy-start.4 = (bf16[144,2640]{1,0:T(8,128)(2,1)S(1)}, bf16[144,2640]{1,0:T(8,128)(2,1)}, u32[]{:S(2)}) copy-start(bf16[144,2640]{1,0:T(8,128)(2,1)} %param.8) | copy-start | bytes 2280964
  9.1 12.0 %all-to-all-start = ((s32[8,2,2,6]{3,2,1,0:T(2,128)}), s32[8,2,2,6]{3,2,1,0:T(2,128)S(1)}, u32[]{:S(2)}, u32[]{:S(2)}) async-start(s32[8,2,2,6]{3,2,1,0:T(2,128)} %copy.71), calls=%async_computation | async-start | bytes 32768 | tf_op jit(solution)/shard_map/all_to_all | solution.py:264
  15.5 144.0 %all-gather.9.cloned.1.call-start = ((), (), s32[]{:S(2)}) async-start(), calls=%async_computation.3 | async-start | bytes 7741440 | tf_op jit(solution)/shard_map/all_gather | solution.py:239
  15.5 1.3 copy-start.5
  18.0 1.2 copy-start.7
  21.1 21.4 %all-to-all-start.1 = ((bf16[8,2,18,660]{3,1,2,0:T(2,128)(2,1)}), bf16[8,2,18,660]{3,1,2,0:T(2,128)(2,1)S(1)}, u32[]{:S(2)}, u32[]{:S(2)}) async-start(bf16[8,2,18,660]{3,1,2,0:T(2,128)(2,1)} %copy.78), calls=%async_computation.1 | async-start | bytes 884736 | tf_op jit(solution)/shard_map/all_to_all | solution.py:281
  71.3 5.4 %collective-permute-start = (f32[144]{0:T(256)S(1)}, f32[144]{0:T(256)S(1)}, u32[]{:S(2)}, u32[]{:S(2)}) collective-permute-start(f32[144]{0:T(256)S(1)} %fusion.3), channel_id=1, source_target_pairs={{0,16},{4,20},{8,24},{12,28},{16,0},{20,4},{24,8},{28,12},{1,17},{... | collective-permute-start | bytes 1736 | tf_op jit(solution)/shard_map/ppermute | solution.py:158
  76.8 6.3 %copy-start.1 = (bf16[72,1320]{1,0:T(8,128)(2,1)}, bf16[72,1320]{1,0:T(8,128)(2,1)S(1)}, u32[]{:S(2)}) copy-start(bf16[72,1320]{1,0:T(8,128)(2,1)S(1)} %convolution_convert_fusion.6) | copy-start | bytes 570244
  77.6 7.9 %copy-start.3 = (bf16[72,2640]{1,0:T(8,128)(2,1)S(1)}, bf16[72,2640]{1,0:T(8,128)(2,1)}, u32[]{:S(2)}) copy-start(bf16[72,2640]{1,0:T(8,128)(2,1)} %convolution_convert_fusion.3) | copy-start | bytes 1140484
  83.1 22.9 %collective-permute-start.1 = (bf16[72,2240]{1,0:T(8,128)(2,1)S(1)}, bf16[72,2240]{1,0:T(8,128)(2,1)S(1)}, u32[]{:S(2)}, u32[]{:S(2)}) collective-permute-start(bf16[72,2240]{1,0:T(8,128)(2,1)S(1)} %slice.297), channel_id=1, source_target_pairs={{0,16},{4,20},{8,24},{12,28},{16,0},{20,4},{24,8},{28,12},{1,17},{... | collective-permute-start | bytes 967688 | tf_op jit(solution)/shard_map/ppermute | solution.py:158
  85.7 25.6 %collective-permute-start.6 = (bf16[72,1320]{1,0:T(8,128)(2,1)S(1)}, bf16[72,1320]{1,0:T(8,128)(2,1)S(1)}, u32[]{:S(2)}, u32[]{:S(2)}) collective-permute-start(bf16[72,1320]{1,0:T(8,128)(2,1)S(1)} %get-tuple-element.42), channel_id=1, source_target_pairs={{0,16},{4,20},{8,24},{12,28},{16,0},{20,4},{24,8},{28,12},{1,17},{... | collective-permute-start | bytes 570248 | tf_op jit(solution)/shard_map/ppermute | solution.py:158
  106.2 53.3 %collective-permute-start.2 = (bf16[72,2240]{1,0:T(8,128)(2,1)S(1)}, bf16[72,2240]{1,0:T(8,128)(2,1)}, u32[]{:S(2)}, u32[]{:S(2)}) collective-permute-start(bf16[72,2240]{1,0:T(8,128)(2,1)S(1)} %multiply_convert_fusion.1), channel_id=1, source_target_pairs={{0,16},{4,20},{8,24},{12,28},{16,0},{20,4},{24,8},{28,12},{1,17},{... | collective-permute-start | bytes 967688 | tf_op jit(solution)/shard_map/ppermute | solution.py:158
  185.7 8.1 %copy-start.2 = (bf16[72,1320]{1,0:T(8,128)(2,1)S(1)}, bf16[72,1320]{1,0:T(8,128)(2,1)}, u32[]{:S(2)}) copy-start(bf16[72,1320]{1,0:T(8,128)(2,1)} %copy-done.1) | copy-start | bytes 570244
  185.7 7.9 %collective-permute-start.3 = (f32[144]{0:T(256)S(1)}, f32[144]{0:T(256)S(1)}, u32[]{:S(2)}, u32[]{:S(2)}) collective-permute-start(f32[144]{0:T(256)S(1)} %get-tuple-element.11), channel_id=1, source_target_pairs={{0,16},{4,20},{8,24},{12,28},{16,0},{20,4},{24,8},{28,12},{1,17},{... | collective-permute-start | bytes 1736 | tf_op jit(solution)/shard_map/ppermute | solution.py:158
  190.7 26.1 %collective-permute-start.7 = (bf16[72,2240]{1,0:T(8,128)(2,1)}, bf16[72,2240]{1,0:T(8,128)(2,1)}, u32[]{:S(2)}, u32[]{:S(2)}) collective-permute-start(bf16[72,2240]{1,0:T(8,128)(2,1)} %slice.295), channel_id=1, source_target_pairs={{0,16},{4,20},{8,24},{12,28},{16,0},{20,4},{24,8},{28,12},{1,17},{... | collective-permute-start | bytes 967688 | tf_op jit(solution)/shard_map/ppermute | solution.py:158
  201.1 21.3 %collective-permute-start.4 = (bf16[72,2240]{1,0:T(8,128)(2,1)S(1)}, bf16[72,2240]{1,0:T(8,128)(2,1)S(1)}, u32[]{:S(2)}, u32[]{:S(2)}) collective-permute-start(bf16[72,2240]{1,0:T(8,128)(2,1)S(1)} %slice.296), channel_id=1, source_target_pairs={{0,16},{4,20},{8,24},{12,28},{16,0},{20,4},{24,8},{28,12},{1,17},{... | collective-permute-start | bytes 967688 | tf_op jit(solution)/shard_map/ppermute | solution.py:158
  224.6 32.4 %collective-permute-start.8 = (bf16[72,2240]{1,0:T(8,128)(2,1)}, bf16[72,2240]{1,0:T(8,128)(2,1)S(1)}, u32[]{:S(2)}, u32[]{:S(2)}) collective-permute-start(bf16[72,2240]{1,0:T(8,128)(2,1)} %get-tuple-element.24), channel_id=1, source_target_pairs={{0,16},{4,20},{8,24},{12,28},{16,0},{20,4},{24,8},{28,12},{1,17},{... | collective-permute-start | bytes 967688 | tf_op jit(solution)/shard_map/ppermute | solution.py:158
  225.7 80.1 %collective-permute-start.10 = (bf16[144,1320]{1,0:T(8,128)(2,1)}, bf16[144,1320]{1,0:T(8,128)(2,1)}, u32[]{:S(2)}, u32[]{:S(2)}) collective-permute-start(bf16[144,1320]{1,0:T(8,128)(2,1)} %slice.221), channel_id=1, source_target_pairs={{0,16},{4,20},{8,24},{12,28},{16,0},{20,4},{24,8},{28,12},{1,17},{... | collective-permute-start | bytes 1140488 | tf_op jit(solution)/shard_map/ppermute | solution.py:158
  228.6 44.2 %collective-permute-start.5 = (bf16[72,2240]{1,0:T(8,128)(2,1)}, bf16[72,2240]{1,0:T(8,128)(2,1)}, u32[]{:S(2)}, u32[]{:S(2)}) collective-permute-start(bf16[72,2240]{1,0:T(8,128)(2,1)} %get-tuple-element.23), channel_id=1, source_target_pairs={{0,16},{4,20},{8,24},{12,28},{16,0},{20,4},{24,8},{28,12},{1,17},{... | collective-permute-start | bytes 967688 | tf_op jit(solution)/shard_map/ppermute | solution.py:158
  262.0 10.8 %copy-start.6 = (bf16[72,2240]{1,0:T(8,128)(2,1)S(1)}, bf16[72,2240]{1,0:T(8,128)(2,1)}, u32[]{:S(2)}) copy-start(bf16[72,2240]{1,0:T(8,128)(2,1)} %get-tuple-element.23) | copy-start | bytes 967684
  305.7 18.5 %collective-permute-start.9 = (bf16[144,1320]{1,0:T(8,128)(2,1)S(1)}, bf16[144,1320]{1,0:T(8,128)(2,1)S(1)}, u32[]{:S(2)}, u32[]{:S(2)}) collective-permute-start(bf16[144,1320]{1,0:T(8,128)(2,1)S(1)} %pad_maximum_fusion.4), channel_id=1, source_target_pairs={{0,16},{4,20},{8,24},{12,28},{16,0},{20,4},{24,8},{28,12},{1,17},{... | collective-permute-start | bytes 1140488 | tf_op jit(solution)/shard_map/ppermute | solution.py:158
  (1 other events, 0.8 us)
Sparse Core Ops, SparseCore 0:
  9.6 69.4 all-gather.6
  80.6 78.8 all-gather.8
